TPU v7x, 512 devices: a whole 4x4x16 slice. The times are simulated.
512 devices in a mesh: sweep: 8 (over z_lo), tile: 64 (over z_hi, y, x, core).
Axes of the slice: x: 4, y: 4, z: 16 (z_hi: 2, z_lo: 8; z = z_hi * 8 + z_lo), core: 2. Of those that a mesh axis runs over, the one named last changes fastest.
Arguments:
- adjoint_source: bfloat16 [2, 8, 256, 128, 256], P(None, 'sweep', 'tile'), may hold values from -6 to 6
- forward_field: bfloat16 [2, 8, 256, 128, 256], P(None, 'sweep', 'tile'), may hold values from -6 to 6
- factor_blocks: bfloat16 [8, 256, 3, 2, 128, 128], P('sweep', 'tile')
- factor_index: int32 [8, 256, 3], P('sweep', 'tile'), may hold values from 0 to 7, as said below
- pml_thickness: int32 [256], replicated, may hold values from 1 to 4
Outputs:
- adjoint_field: bfloat16 [2, 8, 256, 128, 256], P(None, 'sweep', 'tile')
- gradient: float32 [8, 256, 128], P('sweep', 'tile')
Inputs may be any that keep to these rules, and one draw needn't show every extreme that they name: `factor_index`: each row's 3 numbers differ; the first is 2 + (x mod 4), the row itself, and the second lies among the 2 rows beyond the device's rows on either side.
All inputs are finite; a program needn't handle non-finite values.
Results may differ from a plain program's by a relative error of at most 0.015.
Values may be sent and summed in bfloat16 or wider, within the bound.
A program may use at most 64 MiB of HBM per device.

v0:
```python
import math

import jax
import jax.numpy as jnp
from jax import lax
from jax.sharding import PartitionSpec as P

REACH = 2


lateral_weight = 0.25
pml_factor = 0.55


def with_halo(cells, sides, width):
    for axis, dim in sides:
        count = lax.axis_size(axis)
        ends = count - 1
        head = lax.slice_in_dim(cells, 0, width, axis=dim)
        tail = lax.slice_in_dim(cells, cells.shape[dim] - width, cells.shape[dim], axis=dim)
        cells = jnp.concatenate(
            [
                lax.ppermute(tail, axis, [(i, (i + 1) % count) for i in range(ends)]),
                cells,
                lax.ppermute(head, axis, [((i + 1) % count, i) for i in range(ends)]),
            ],
            axis=dim,
        )
    return cells


def shifted(array, axis, by):
    size = lax.axis_size(axis)
    pairs = [(i, i + by) for i in range(size) if 0 <= i + by < size]
    return lax.ppermute(array, axis, pairs)


def laplace(extended):
    center = extended[:, 1:-1]
    padded = jnp.pad(center, ((0, 0), (0, 0), (1, 1), (0, 0)))
    return extended[:, 2:] + extended[:, :-2] + padded[:, :, 2:] + padded[:, :, :-2] - 4.0 * center


def factor_apply(blocks, indices, extended_w):
    picked = jnp.take(extended_w, indices, axis=1)
    terms = jnp.einsum("tkcij,dtkjr->cdtir", blocks, picked, preferred_element_type=jnp.float32)
    real_part = terms[0, 0] - terms[1, 1]
    imag_part = terms[0, 1] + terms[1, 0]
    return jnp.stack([real_part, imag_part]).astype(jnp.bfloat16)


def layer_step(incoming, source_layer, blocks, indices, layer_gain):
    extended = with_halo(incoming, (("tile", 1),), 1).astype(jnp.float32)
    own_w = (
        source_layer.astype(jnp.float32)
        - layer_gain * (extended[:, 1:-1] + lateral_weight * laplace(extended))
    ).astype(jnp.bfloat16)
    extended_w = with_halo(own_w, (("tile", 1),), REACH)
    return factor_apply(blocks, indices, extended_w)


def on_device(adjoint_source, forward_field, factor_blocks, factor_index, pml_thickness):
    sweeps = lax.axis_size("sweep")
    position = lax.axis_index("sweep")
    layers = adjoint_source.shape[1]
    columns = adjoint_source.shape[4]
    depth_z = layers * sweeps
    norm_scale = 1.0 / math.sqrt(columns)
    groups = 1
    group_width = columns // groups

    def run_section(step_idx, state):
        handed, adjoint, gradient = state
        incoming = shifted(handed, "sweep", -1)
        group_idx = step_idx - (sweeps - 1 - position)
        is_valid = (group_idx >= 0) & (group_idx < groups)
        current = incoming
        for layer_idx in reversed(range(layers)):
            depth_pos = position * layers + layer_idx
            in_pml = (depth_pos < pml_thickness) | (depth_pos >= depth_z - pml_thickness)
            layer_gain = jnp.where(in_pml, pml_factor, 1.0).astype(jnp.float32)
            source_layer = adjoint_source[:, layer_idx]
            current = layer_step(
                current, source_layer, factor_blocks[layer_idx], factor_index[layer_idx], layer_gain
            )
            stored = adjoint[:, layer_idx]
            update = jnp.where(is_valid, current, stored)[:, None]
            adjoint = update
            forward_slice = forward_field[:, layer_idx]
            contribution = (
                jnp.sum(
                    forward_slice.astype(jnp.float32) * current.astype(jnp.float32), axis=(0, 3)
                )
                * norm_scale
            )
            gradient = gradient.at[layer_idx].add(jnp.where(is_valid, contribution, 0.0))
        return (current, adjoint, gradient)

    handed = jnp.zeros(
        (2, adjoint_source.shape[2], adjoint_source.shape[3], group_width), jnp.bfloat16
    )
    adjoint = jnp.zeros(adjoint_source.shape, jnp.bfloat16)
    gradient = jnp.zeros((layers, adjoint_source.shape[2], adjoint_source.shape[3]), jnp.float32)
    _, adjoint, gradient = lax.fori_loop(
        0, groups + sweeps - 1, run_section, (handed, adjoint, gradient)
    )
    return (adjoint, gradient)


def solution(mesh):
    placed = (
        P(None, "sweep", "tile", None, None),
        P(None, "sweep", "tile", None, None),
        P("sweep", "tile", None, None, None, None),
        P("sweep", "tile", None),
        P(),
    )
    return jax.shard_map(
        on_device,
        mesh=mesh,
        in_specs=placed,
        out_specs=(P(None, "sweep", "tile", None, None), P("sweep", "tile", None)),
        check_vma=False,
    )
```

profile of v0, /device:TPU:448, one launch (start us, length us, event | category | flops | bytes accessed | tf_op | source)
XLA Modules:
  0.0 531.2 jit_solution(8438312856347716915)
XLA Ops:
  4.2 525.0 %while.22 = (s32[]{:T(128)}, bf16[2,4,128,256]{2,3,1,0:T(8,128)(2,1)S(1)}, bf16[2,1,4,128,256]{3,4,0,1,2:T(8,128)(2,1)}, f32[1,4,128]{2,1,0:T(4,128)S(1)}, s32[1...) while((s32[]{:T(128)}, ...), condition=%wide.region_2.3_spmd.clone, body=%wide.region_0.2_spmd.clone.sunk | while | flops 411176800 | bytes 37240816 | solution.py:104
  4.3 2.9 collective-permute-start
  7.4 12.4 %collective-permute-done = bf16[2,4,128,256]{2,3,1,0:T(8,128)(2,1)S(1)} collective-permute-done((bf16[2,4,128,256]{2,3,1,0:T(8,128)(2,1)S(1)}, bf16[2,4,128,256]{2,3,1,0:T(8,128)(2,1)S(1)}, u32[]{:S(2)}, u32[]{:S(2)}) %collective-permute-start) | collective-permute-done | bytes 524320 | tf_op jit(solution)/shard_map/while/body/eval_jaxpr/ppermute | solution.py:35
  19.8 8.7 %collective-permute-start.1 = (bf16[2,1,128,256]{2,3,1,0:T(8,128)(2,1)S(1)}, bf16[2,1,128,256]{2,3,1,0:T(8,128)(2,1)S(1)}, u32[]{:S(2)}, u32[]{:S(2)}) collective-permute-start(bf16[2,1,128,256]{2,3,1,0:T(8,128)(2,1)S(1)} %get-tuple-element.474), channel_id=1, source_target_pairs={{1,0},{2,1},{3,2},{4,3},{5,4},{6,5},{7,6},{8,7},{9,8},{10,9},{11,1... | collective-permute-start | bytes 393224 | tf_op jit(solution)/shard_map/while/body/eval_jaxpr/ppermute | solution.py:25
  32.8 16.8 %collective-permute-done.2 = bf16[2,1,128,256]{2,3,1,0:T(8,128)(2,1)S(1)} collective-permute-done((bf16[2,1,128,256]{2,3,1,0:T(8,128)(2,1)S(1)}, bf16[2,1,128,256]{2,3,1,0:T(8,128)(2,1)S(1)}, u32[]{:S(2)}, u32[]{:S(2)}) %collective-permute-start.2) | collective-permute-done | bytes 131104 | tf_op jit(solution)/shard_map/while/body/eval_jaxpr/ppermute | solution.py:23
  52.4 2.4 collective-permute-start.4
  55.0 5.6 %collective-permute-done.3 = bf16[2,2,128,256]{2,3,1,0:T(8,128)(2,1)S(1)} collective-permute-done((bf16[2,2,128,256]{2,3,1,0:T(8,128)(2,1)S(1)}, bf16[2,2,128,256]{2,3,1,0:T(8,128)(2,1)S(1)}, u32[]{:S(2)}, u32[]{:S(2)}) %collective-permute-start.3) | collective-permute-done | bytes 262176 | tf_op jit(solution)/shard_map/while/body/eval_jaxpr/ppermute | solution.py:25
  60.6 16.8 %collective-permute-done.4 = bf16[2,2,128,256]{2,3,1,0:T(8,128)(2,1)S(1)} collective-permute-done((bf16[2,2,128,256]{2,3,1,0:T(8,128)(2,1)S(1)}, bf16[2,2,128,256]{2,3,1,0:T(8,128)(2,1)S(1)}, u32[]{:S(2)}, u32[]{:S(2)}) %collective-permute-start.4) | collective-permute-done | bytes 262176 | tf_op jit(solution)/shard_map/while/body/eval_jaxpr/ppermute | solution.py:23
  84.3 9.0 %collective-permute-done = bf16[2,4,128,256]{2,3,1,0:T(8,128)(2,1)S(1)} collective-permute-done((bf16[2,4,128,256]{2,3,1,0:T(8,128)(2,1)S(1)}, bf16[2,4,128,256]{2,3,1,0:T(8,128)(2,1)S(1)}, u32[]{:S(2)}, u32[]{:S(2)}) %collective-permute-start) | collective-permute-done | bytes 524320 | tf_op jit(solution)/shard_map/while/body/eval_jaxpr/ppermute | solution.py:35
  97.7 16.7 %collective-permute-done.2 = bf16[2,1,128,256]{2,3,1,0:T(8,128)(2,1)S(1)} collective-permute-done((bf16[2,1,128,256]{2,3,1,0:T(8,128)(2,1)S(1)}, bf16[2,1,128,256]{2,3,1,0:T(8,128)(2,1)S(1)}, u32[]{:S(2)}, u32[]{:S(2)}) %collective-permute-start.2) | collective-permute-done | bytes 131104 | tf_op jit(solution)/shard_map/while/body/eval_jaxpr/ppermute | solution.py:23
  119.8 2.5 collective-permute-done.3
  122.3 16.8 %collective-permute-done.4 = bf16[2,2,128,256]{2,3,1,0:T(8,128)(2,1)S(1)} collective-permute-done((bf16[2,2,128,256]{2,3,1,0:T(8,128)(2,1)S(1)}, bf16[2,2,128,256]{2,3,1,0:T(8,128)(2,1)S(1)}, u32[]{:S(2)}, u32[]{:S(2)}) %collective-permute-start.4) | collective-permute-done | bytes 262176 | tf_op jit(solution)/shard_map/while/body/eval_jaxpr/ppermute | solution.py:23
  143.9 4.9 collective-permute-start
  149.0 6.5 %collective-permute-done = bf16[2,4,128,256]{2,3,1,0:T(8,128)(2,1)S(1)} collective-permute-done((bf16[2,4,128,256]{2,3,1,0:T(8,128)(2,1)S(1)}, bf16[2,4,128,256]{2,3,1,0:T(8,128)(2,1)S(1)}, u32[]{:S(2)}, u32[]{:S(2)}) %collective-permute-start) | collective-permute-done | bytes 524320 | tf_op jit(solution)/shard_map/while/body/eval_jaxpr/ppermute | solution.py:35
  157.4 2.4 collective-permute-start.2
  159.9 16.7 %collective-permute-done.2 = bf16[2,1,128,256]{2,3,1,0:T(8,128)(2,1)S(1)} collective-permute-done((bf16[2,1,128,256]{2,3,1,0:T(8,128)(2,1)S(1)}, bf16[2,1,128,256]{2,3,1,0:T(8,128)(2,1)S(1)}, u32[]{:S(2)}, u32[]{:S(2)}) %collective-permute-start.2) | collective-permute-done | bytes 131104 | tf_op jit(solution)/shard_map/while/body/eval_jaxpr/ppermute | solution.py:23
  179.5 2.4 collective-permute-start.4
  182.0 5.6 %collective-permute-done.3 = bf16[2,2,128,256]{2,3,1,0:T(8,128)(2,1)S(1)} collective-permute-done((bf16[2,2,128,256]{2,3,1,0:T(8,128)(2,1)S(1)}, bf16[2,2,128,256]{2,3,1,0:T(8,128)(2,1)S(1)}, u32[]{:S(2)}, u32[]{:S(2)}) %collective-permute-start.3) | collective-permute-done | bytes 262176 | tf_op jit(solution)/shard_map/while/body/eval_jaxpr/ppermute | solution.py:25
  187.7 16.8 %collective-permute-done.4 = bf16[2,2,128,256]{2,3,1,0:T(8,128)(2,1)S(1)} collective-permute-done((bf16[2,2,128,256]{2,3,1,0:T(8,128)(2,1)S(1)}, bf16[2,2,128,256]{2,3,1,0:T(8,128)(2,1)S(1)}, u32[]{:S(2)}, u32[]{:S(2)}) %collective-permute-start.4) | collective-permute-done | bytes 262176 | tf_op jit(solution)/shard_map/while/body/eval_jaxpr/ppermute | solution.py:23
  211.4 8.9 %collective-permute-done = bf16[2,4,128,256]{2,3,1,0:T(8,128)(2,1)S(1)} collective-permute-done((bf16[2,4,128,256]{2,3,1,0:T(8,128)(2,1)S(1)}, bf16[2,4,128,256]{2,3,1,0:T(8,128)(2,1)S(1)}, u32[]{:S(2)}, u32[]{:S(2)}) %collective-permute-start) | collective-permute-done | bytes 524320 | tf_op jit(solution)/shard_map/while/body/eval_jaxpr/ppermute | solution.py:35
  222.3 2.4 collective-permute-start.2
  225.1 16.8 %collective-permute-done.2 = bf16[2,1,128,256]{2,3,1,0:T(8,128)(2,1)S(1)} collective-permute-done((bf16[2,1,128,256]{2,3,1,0:T(8,128)(2,1)S(1)}, bf16[2,1,128,256]{2,3,1,0:T(8,128)(2,1)S(1)}, u32[]{:S(2)}, u32[]{:S(2)}) %collective-permute-start.2) | collective-permute-done | bytes 131104 | tf_op jit(solution)/shard_map/while/body/eval_jaxpr/ppermute | solution.py:23
  244.7 2.4 collective-permute-start.4
  247.2 3.9 collective-permute-done.3
  251.1 16.8 %collective-permute-done.4 = bf16[2,2,128,256]{2,3,1,0:T(8,128)(2,1)S(1)} collective-permute-done((bf16[2,2,128,256]{2,3,1,0:T(8,128)(2,1)S(1)}, bf16[2,2,128,256]{2,3,1,0:T(8,128)(2,1)S(1)}, u32[]{:S(2)}, u32[]{:S(2)}) %collective-permute-start.4) | collective-permute-done | bytes 262176 | tf_op jit(solution)/shard_map/while/body/eval_jaxpr/ppermute | solution.py:23
  272.7 3.1 collective-permute-start
  276.0 7.7 %collective-permute-done = bf16[2,4,128,256]{2,3,1,0:T(8,128)(2,1)S(1)} collective-permute-done((bf16[2,4,128,256]{2,3,1,0:T(8,128)(2,1)S(1)}, bf16[2,4,128,256]{2,3,1,0:T(8,128)(2,1)S(1)}, u32[]{:S(2)}, u32[]{:S(2)}) %collective-permute-start) | collective-permute-done | bytes 524320 | tf_op jit(solution)/shard_map/while/body/eval_jaxpr/ppermute | solution.py:35
  285.7 2.4 collective-permute-start.2
  289.6 16.8 %collective-permute-done.2 = bf16[2,1,128,256]{2,3,1,0:T(8,128)(2,1)S(1)} collective-permute-done((bf16[2,1,128,256]{2,3,1,0:T(8,128)(2,1)S(1)}, bf16[2,1,128,256]{2,3,1,0:T(8,128)(2,1)S(1)}, u32[]{:S(2)}, u32[]{:S(2)}) %collective-permute-start.2) | collective-permute-done | bytes 131104 | tf_op jit(solution)/shard_map/while/body/eval_jaxpr/ppermute | solution.py:23
  309.2 2.4 collective-permute-start.4
  311.7 3.8 collective-permute-done.3
  315.5 16.8 %collective-permute-done.4 = bf16[2,2,128,256]{2,3,1,0:T(8,128)(2,1)S(1)} collective-permute-done((bf16[2,2,128,256]{2,3,1,0:T(8,128)(2,1)S(1)}, bf16[2,2,128,256]{2,3,1,0:T(8,128)(2,1)S(1)}, u32[]{:S(2)}, u32[]{:S(2)}) %collective-permute-start.4) | collective-permute-done | bytes 262176 | tf_op jit(solution)/shard_map/while/body/eval_jaxpr/ppermute | solution.py:23
  339.6 8.6 %collective-permute-done = bf16[2,4,128,256]{2,3,1,0:T(8,128)(2,1)S(1)} collective-permute-done((bf16[2,4,128,256]{2,3,1,0:T(8,128)(2,1)S(1)}, bf16[2,4,128,256]{2,3,1,0:T(8,128)(2,1)S(1)}, u32[]{:S(2)}, u32[]{:S(2)}) %collective-permute-start) | collective-permute-done | bytes 524320 | tf_op jit(solution)/shard_map/while/body/eval_jaxpr/ppermute | solution.py:35
  350.1 2.4 collective-permute-start.2
  353.3 16.8 %collective-permute-done.2 = bf16[2,1,128,256]{2,3,1,0:T(8,128)(2,1)S(1)} collective-permute-done((bf16[2,1,128,256]{2,3,1,0:T(8,128)(2,1)S(1)}, bf16[2,1,128,256]{2,3,1,0:T(8,128)(2,1)S(1)}, u32[]{:S(2)}, u32[]{:S(2)}) %collective-permute-start.2) | collective-permute-done | bytes 131104 | tf_op jit(solution)/shard_map/while/body/eval_jaxpr/ppermute | solution.py:23
  375.4 4.0 collective-permute-done.3
  379.4 16.8 %collective-permute-done.4 = bf16[2,2,128,256]{2,3,1,0:T(8,128)(2,1)S(1)} collective-permute-done((bf16[2,2,128,256]{2,3,1,0:T(8,128)(2,1)S(1)}, bf16[2,2,128,256]{2,3,1,0:T(8,128)(2,1)S(1)}, u32[]{:S(2)}, u32[]{:S(2)}) %collective-permute-start.4) | collective-permute-done | bytes 262176 | tf_op jit(solution)/shard_map/while/body/eval_jaxpr/ppermute | solution.py:23
  401.0 2.8 collective-permute-start
  404.0 8.1 %collective-permute-done = bf16[2,4,128,256]{2,3,1,0:T(8,128)(2,1)S(1)} collective-permute-done((bf16[2,4,128,256]{2,3,1,0:T(8,128)(2,1)S(1)}, bf16[2,4,128,256]{2,3,1,0:T(8,128)(2,1)S(1)}, u32[]{:S(2)}, u32[]{:S(2)}) %collective-permute-start) | collective-permute-done | bytes 524320 | tf_op jit(solution)/shard_map/while/body/eval_jaxpr/ppermute | solution.py:35
  414.0 2.4 collective-permute-start.2
  417.6 16.8 %collective-permute-done.2 = bf16[2,1,128,256]{2,3,1,0:T(8,128)(2,1)S(1)} collective-permute-done((bf16[2,1,128,256]{2,3,1,0:T(8,128)(2,1)S(1)}, bf16[2,1,128,256]{2,3,1,0:T(8,128)(2,1)S(1)}, u32[]{:S(2)}, u32[]{:S(2)}) %collective-permute-start.2) | collective-permute-done | bytes 131104 | tf_op jit(solution)/shard_map/while/body/eval_jaxpr/ppermute | solution.py:23
  439.8 3.8 collective-permute-done.3
  443.6 16.8 %collective-permute-done.4 = bf16[2,2,128,256]{2,3,1,0:T(8,128)(2,1)S(1)} collective-permute-done((bf16[2,2,128,256]{2,3,1,0:T(8,128)(2,1)S(1)}, bf16[2,2,128,256]{2,3,1,0:T(8,128)(2,1)S(1)}, u32[]{:S(2)}, u32[]{:S(2)}) %collective-permute-start.4) | collective-permute-done | bytes 262176 | tf_op jit(solution)/shard_map/while/body/eval_jaxpr/ppermute | solution.py:23
  465.2 2.5 collective-permute-start
  467.9 8.3 %collective-permute-done = bf16[2,4,128,256]{2,3,1,0:T(8,128)(2,1)S(1)} collective-permute-done((bf16[2,4,128,256]{2,3,1,0:T(8,128)(2,1)S(1)}, bf16[2,4,128,256]{2,3,1,0:T(8,128)(2,1)S(1)}, u32[]{:S(2)}, u32[]{:S(2)}) %collective-permute-start) | collective-permute-done | bytes 524320 | tf_op jit(solution)/shard_map/while/body/eval_jaxpr/ppermute | solution.py:35
  481.6 16.8 %collective-permute-done.2 = bf16[2,1,128,256]{2,3,1,0:T(8,128)(2,1)S(1)} collective-permute-done((bf16[2,1,128,256]{2,3,1,0:T(8,128)(2,1)S(1)}, bf16[2,1,128,256]{2,3,1,0:T(8,128)(2,1)S(1)}, u32[]{:S(2)}, u32[]{:S(2)}) %collective-permute-start.2) | collective-permute-done | bytes 131104 | tf_op jit(solution)/shard_map/while/body/eval_jaxpr/ppermute | solution.py:23
  503.7 3.9 collective-permute-done.3
  507.6 16.8 %collective-permute-done.4 = bf16[2,2,128,256]{2,3,1,0:T(8,128)(2,1)S(1)} collective-permute-done((bf16[2,2,128,256]{2,3,1,0:T(8,128)(2,1)S(1)}, bf16[2,2,128,256]{2,3,1,0:T(8,128)(2,1)S(1)}, u32[]{:S(2)}, u32[]{:S(2)}) %collective-permute-start.4) | collective-permute-done | bytes 262176 | tf_op jit(solution)/shard_map/while/body/eval_jaxpr/ppermute | solution.py:23
  (250 shorter events, 112.1 us)
Async XLA Ops:
  0.6 2.2 copy-start.3
  0.6 2.5 copy-start.4
  2.9 1.4 copy-start.5
  2.9 1.4 copy-start.7
  4.3 15.6 %collective-permute-start = (bf16[2,4,128,256]{2,3,1,0:T(8,128)(2,1)S(1)}, bf16[2,4,128,256]{2,3,1,0:T(8,128)(2,1)S(1)}, u32[]{:S(2)}, u32[]{:S(2)}) collective-permute-start(bf16[2,4,128,256]{2,3,1,0:T(8,128)(2,1)S(1)} %get-tuple-element.496), channel_id=1, source_target_pairs={{64,0},{128,64},{192,128},{256,192},{320,256},{384,320},{448,384},... | collective-permute-start | bytes 1572872 | tf_op jit(solution)/shard_map/while/body/eval_jaxpr/ppermute | solution.py:35
  19.8 13.0 %collective-permute-start.1 = (bf16[2,1,128,256]{2,3,1,0:T(8,128)(2,1)S(1)}, bf16[2,1,128,256]{2,3,1,0:T(8,128)(2,1)S(1)}, u32[]{:S(2)}, u32[]{:S(2)}) collective-permute-start(bf16[2,1,128,256]{2,3,1,0:T(8,128)(2,1)S(1)} %get-tuple-element.474), channel_id=1, source_target_pairs={{1,0},{2,1},{3,2},{4,3},{5,4},{6,5},{7,6},{8,7},{9,8},{10,9},{11,1... | collective-permute-start | bytes 393224 | tf_op jit(solution)/shard_map/while/body/eval_jaxpr/ppermute | solution.py:25
  28.5 21.1 %collective-permute-start.2 = (bf16[2,1,128,256]{2,3,1,0:T(8,128)(2,1)S(1)}, bf16[2,1,128,256]{2,3,1,0:T(8,128)(2,1)S(1)}, u32[]{:S(2)}, u32[]{:S(2)}) collective-permute-start(bf16[2,1,128,256]{2,3,1,0:T(8,128)(2,1)S(1)} %get-tuple-element.475), channel_id=1, source_target_pairs={{0,1},{1,2},{2,3},{3,4},{4,5},{5,6},{6,7},{7,8},{8,9},{9,10},{10,1... | collective-permute-start | bytes 393224 | tf_op jit(solution)/shard_map/while/body/eval_jaxpr/ppermute | solution.py:23
  50.5 10.1 %collective-permute-start.3 = (bf16[2,2,128,256]{2,3,1,0:T(8,128)(2,1)S(1)}, bf16[2,2,128,256]{2,3,1,0:T(8,128)(2,1)S(1)}, u32[]{:S(2)}, u32[]{:S(2)}) collective-permute-start(bf16[2,2,128,256]{2,3,1,0:T(8,128)(2,1)S(1)} %get-tuple-element.476), channel_id=1, source_target_pairs={{1,0},{2,1},{3,2},{4,3},{5,4},{6,5},{7,6},{8,7},{9,8},{10,9},{11,1... | collective-permute-start | bytes 786440 | tf_op jit(solution)/shard_map/while/body/eval_jaxpr/ppermute | solution.py:25
  52.4 24.9 %collective-permute-start.4 = (bf16[2,2,128,256]{2,3,1,0:T(8,128)(2,1)S(1)}, bf16[2,2,128,256]{2,3,1,0:T(8,128)(2,1)S(1)}, u32[]{:S(2)}, u32[]{:S(2)}) collective-permute-start(bf16[2,2,128,256]{2,3,1,0:T(8,128)(2,1)S(1)} %get-tuple-element.477), channel_id=1, source_target_pairs={{0,1},{1,2},{2,3},{3,4},{4,5},{5,6},{6,7},{7,8},{8,9},{9,10},{10,1... | collective-permute-start | bytes 786440 | tf_op jit(solution)/shard_map/while/body/eval_jaxpr/ppermute | solution.py:23
  80.2 1.2 copy-start
  82.2 11.1 %collective-permute-start = (bf16[2,4,128,256]{2,3,1,0:T(8,128)(2,1)S(1)}, bf16[2,4,128,256]{2,3,1,0:T(8,128)(2,1)S(1)}, u32[]{:S(2)}, u32[]{:S(2)}) collective-permute-start(bf16[2,4,128,256]{2,3,1,0:T(8,128)(2,1)S(1)} %get-tuple-element.496), channel_id=1, source_target_pairs={{64,0},{128,64},{192,128},{256,192},{320,256},{384,320},{448,384},... | collective-permute-start | bytes 1572872 | tf_op jit(solution)/shard_map/while/body/eval_jaxpr/ppermute | solution.py:35
  93.3 4.4 collective-permute-start.1
  95.2 19.2 %collective-permute-start.2 = (bf16[2,1,128,256]{2,3,1,0:T(8,128)(2,1)S(1)}, bf16[2,1,128,256]{2,3,1,0:T(8,128)(2,1)S(1)}, u32[]{:S(2)}, u32[]{:S(2)}) collective-permute-start(bf16[2,1,128,256]{2,3,1,0:T(8,128)(2,1)S(1)} %get-tuple-element.475), channel_id=1, source_target_pairs={{0,1},{1,2},{2,3},{3,4},{4,5},{5,6},{6,7},{7,8},{8,9},{9,10},{10,1... | collective-permute-start | bytes 393224 | tf_op jit(solution)/shard_map/while/body/eval_jaxpr/ppermute | solution.py:23
  115.3 6.9 %collective-permute-start.3 = (bf16[2,2,128,256]{2,3,1,0:T(8,128)(2,1)S(1)}, bf16[2,2,128,256]{2,3,1,0:T(8,128)(2,1)S(1)}, u32[]{:S(2)}, u32[]{:S(2)}) collective-permute-start(bf16[2,2,128,256]{2,3,1,0:T(8,128)(2,1)S(1)} %get-tuple-element.476), channel_id=1, source_target_pairs={{1,0},{2,1},{3,2},{4,3},{5,4},{6,5},{7,6},{8,7},{9,8},{10,9},{11,1... | collective-permute-start | bytes 786440 | tf_op jit(solution)/shard_map/while/body/eval_jaxpr/ppermute | solution.py:25
  117.3 21.8 %collective-permute-start.4 = (bf16[2,2,128,256]{2,3,1,0:T(8,128)(2,1)S(1)}, bf16[2,2,128,256]{2,3,1,0:T(8,128)(2,1)S(1)}, u32[]{:S(2)}, u32[]{:S(2)}) collective-permute-start(bf16[2,2,128,256]{2,3,1,0:T(8,128)(2,1)S(1)} %get-tuple-element.477), channel_id=1, source_target_pairs={{0,1},{1,2},{2,3},{3,4},{4,5},{5,6},{6,7},{7,8},{8,9},{9,10},{10,1... | collective-permute-start | bytes 786440 | tf_op jit(solution)/shard_map/while/body/eval_jaxpr/ppermute | solution.py:23
  141.9 1.2 copy-start
  143.9 11.6 %collective-permute-start = (bf16[2,4,128,256]{2,3,1,0:T(8,128)(2,1)S(1)}, bf16[2,4,128,256]{2,3,1,0:T(8,128)(2,1)S(1)}, u32[]{:S(2)}, u32[]{:S(2)}) collective-permute-start(bf16[2,4,128,256]{2,3,1,0:T(8,128)(2,1)S(1)} %get-tuple-element.496), channel_id=1, source_target_pairs={{64,0},{128,64},{192,128},{256,192},{320,256},{384,320},{448,384},... | collective-permute-start | bytes 1572872 | tf_op jit(solution)/shard_map/while/body/eval_jaxpr/ppermute | solution.py:35
  155.5 4.4 collective-permute-start.1
  157.4 19.2 %collective-permute-start.2 = (bf16[2,1,128,256]{2,3,1,0:T(8,128)(2,1)S(1)}, bf16[2,1,128,256]{2,3,1,0:T(8,128)(2,1)S(1)}, u32[]{:S(2)}, u32[]{:S(2)}) collective-permute-start(bf16[2,1,128,256]{2,3,1,0:T(8,128)(2,1)S(1)} %get-tuple-element.475), channel_id=1, source_target_pairs={{0,1},{1,2},{2,3},{3,4},{4,5},{5,6},{6,7},{7,8},{8,9},{9,10},{10,1... | collective-permute-start | bytes 393224 | tf_op jit(solution)/shard_map/while/body/eval_jaxpr/ppermute | solution.py:23
  177.6 10.1 %collective-permute-start.3 = (bf16[2,2,128,256]{2,3,1,0:T(8,128)(2,1)S(1)}, bf16[2,2,128,256]{2,3,1,0:T(8,128)(2,1)S(1)}, u32[]{:S(2)}, u32[]{:S(2)}) collective-permute-start(bf16[2,2,128,256]{2,3,1,0:T(8,128)(2,1)S(1)} %get-tuple-element.476), channel_id=1, source_target_pairs={{1,0},{2,1},{3,2},{4,3},{5,4},{6,5},{7,6},{8,7},{9,8},{10,9},{11,1... | collective-permute-start | bytes 786440 | tf_op jit(solution)/shard_map/while/body/eval_jaxpr/ppermute | solution.py:25
  179.5 24.9 %collective-permute-start.4 = (bf16[2,2,128,256]{2,3,1,0:T(8,128)(2,1)S(1)}, bf16[2,2,128,256]{2,3,1,0:T(8,128)(2,1)S(1)}, u32[]{:S(2)}, u32[]{:S(2)}) collective-permute-start(bf16[2,2,128,256]{2,3,1,0:T(8,128)(2,1)S(1)} %get-tuple-element.477), channel_id=1, source_target_pairs={{0,1},{1,2},{2,3},{3,4},{4,5},{5,6},{6,7},{7,8},{8,9},{9,10},{10,1... | collective-permute-start | bytes 786440 | tf_op jit(solution)/shard_map/while/body/eval_jaxpr/ppermute | solution.py:23
  209.3 11.1 %collective-permute-start = (bf16[2,4,128,256]{2,3,1,0:T(8,128)(2,1)S(1)}, bf16[2,4,128,256]{2,3,1,0:T(8,128)(2,1)S(1)}, u32[]{:S(2)}, u32[]{:S(2)}) collective-permute-start(bf16[2,4,128,256]{2,3,1,0:T(8,128)(2,1)S(1)} %get-tuple-element.496), channel_id=1, source_target_pairs={{64,0},{128,64},{192,128},{256,192},{320,256},{384,320},{448,384},... | collective-permute-start | bytes 1572872 | tf_op jit(solution)/shard_map/while/body/eval_jaxpr/ppermute | solution.py:35
  220.4 4.7 collective-permute-start.1
  222.3 19.5 %collective-permute-start.2 = (bf16[2,1,128,256]{2,3,1,0:T(8,128)(2,1)S(1)}, bf16[2,1,128,256]{2,3,1,0:T(8,128)(2,1)S(1)}, u32[]{:S(2)}, u32[]{:S(2)}) collective-permute-start(bf16[2,1,128,256]{2,3,1,0:T(8,128)(2,1)S(1)} %get-tuple-element.475), channel_id=1, source_target_pairs={{0,1},{1,2},{2,3},{3,4},{4,5},{5,6},{6,7},{7,8},{8,9},{9,10},{10,1... | collective-permute-start | bytes 393224 | tf_op jit(solution)/shard_map/while/body/eval_jaxpr/ppermute | solution.py:23
  242.8 8.3 %collective-permute-start.3 = (bf16[2,2,128,256]{2,3,1,0:T(8,128)(2,1)S(1)}, bf16[2,2,128,256]{2,3,1,0:T(8,128)(2,1)S(1)}, u32[]{:S(2)}, u32[]{:S(2)}) collective-permute-start(bf16[2,2,128,256]{2,3,1,0:T(8,128)(2,1)S(1)} %get-tuple-element.476), channel_id=1, source_target_pairs={{1,0},{2,1},{3,2},{4,3},{5,4},{6,5},{7,6},{8,7},{9,8},{10,9},{11,1... | collective-permute-start | bytes 786440 | tf_op jit(solution)/shard_map/while/body/eval_jaxpr/ppermute | solution.py:25
  244.7 23.2 %collective-permute-start.4 = (bf16[2,2,128,256]{2,3,1,0:T(8,128)(2,1)S(1)}, bf16[2,2,128,256]{2,3,1,0:T(8,128)(2,1)S(1)}, u32[]{:S(2)}, u32[]{:S(2)}) collective-permute-start(bf16[2,2,128,256]{2,3,1,0:T(8,128)(2,1)S(1)} %get-tuple-element.477), channel_id=1, source_target_pairs={{0,1},{1,2},{2,3},{3,4},{4,5},{5,6},{6,7},{7,8},{8,9},{9,10},{10,1... | collective-permute-start | bytes 786440 | tf_op jit(solution)/shard_map/while/body/eval_jaxpr/ppermute | solution.py:23
  272.7 11.1 %collective-permute-start = (bf16[2,4,128,256]{2,3,1,0:T(8,128)(2,1)S(1)}, bf16[2,4,128,256]{2,3,1,0:T(8,128)(2,1)S(1)}, u32[]{:S(2)}, u32[]{:S(2)}) collective-permute-start(bf16[2,4,128,256]{2,3,1,0:T(8,128)(2,1)S(1)} %get-tuple-element.496), channel_id=1, source_target_pairs={{64,0},{128,64},{192,128},{256,192},{320,256},{384,320},{448,384},... | collective-permute-start | bytes 1572872 | tf_op jit(solution)/shard_map/while/body/eval_jaxpr/ppermute | solution.py:35
  283.8 5.8 %collective-permute-start.1 = (bf16[2,1,128,256]{2,3,1,0:T(8,128)(2,1)S(1)}, bf16[2,1,128,256]{2,3,1,0:T(8,128)(2,1)S(1)}, u32[]{:S(2)}, u32[]{:S(2)}) collective-permute-start(bf16[2,1,128,256]{2,3,1,0:T(8,128)(2,1)S(1)} %get-tuple-element.474), channel_id=1, source_target_pairs={{1,0},{2,1},{3,2},{4,3},{5,4},{6,5},{7,6},{8,7},{9,8},{10,9},{11,1... | collective-permute-start | bytes 393224 | tf_op jit(solution)/shard_map/while/body/eval_jaxpr/ppermute | solution.py:25
  285.7 20.6 %collective-permute-start.2 = (bf16[2,1,128,256]{2,3,1,0:T(8,128)(2,1)S(1)}, bf16[2,1,128,256]{2,3,1,0:T(8,128)(2,1)S(1)}, u32[]{:S(2)}, u32[]{:S(2)}) collective-permute-start(bf16[2,1,128,256]{2,3,1,0:T(8,128)(2,1)S(1)} %get-tuple-element.475), channel_id=1, source_target_pairs={{0,1},{1,2},{2,3},{3,4},{4,5},{5,6},{6,7},{7,8},{8,9},{9,10},{10,1... | collective-permute-start | bytes 393224 | tf_op jit(solution)/shard_map/while/body/eval_jaxpr/ppermute | solution.py:23
  307.3 8.2 %collective-permute-start.3 = (bf16[2,2,128,256]{2,3,1,0:T(8,128)(2,1)S(1)}, bf16[2,2,128,256]{2,3,1,0:T(8,128)(2,1)S(1)}, u32[]{:S(2)}, u32[]{:S(2)}) collective-permute-start(bf16[2,2,128,256]{2,3,1,0:T(8,128)(2,1)S(1)} %get-tuple-element.476), channel_id=1, source_target_pairs={{1,0},{2,1},{3,2},{4,3},{5,4},{6,5},{7,6},{8,7},{9,8},{10,9},{11,1... | collective-permute-start | bytes 786440 | tf_op jit(solution)/shard_map/while/body/eval_jaxpr/ppermute | solution.py:25
  309.2 23.0 %collective-permute-start.4 = (bf16[2,2,128,256]{2,3,1,0:T(8,128)(2,1)S(1)}, bf16[2,2,128,256]{2,3,1,0:T(8,128)(2,1)S(1)}, u32[]{:S(2)}, u32[]{:S(2)}) collective-permute-start(bf16[2,2,128,256]{2,3,1,0:T(8,128)(2,1)S(1)} %get-tuple-element.477), channel_id=1, source_target_pairs={{0,1},{1,2},{2,3},{3,4},{4,5},{5,6},{6,7},{7,8},{8,9},{9,10},{10,1... | collective-permute-start | bytes 786440 | tf_op jit(solution)/shard_map/while/body/eval_jaxpr/ppermute | solution.py:23
  335.1 1.2 copy-start
  337.1 11.1 %collective-permute-start = (bf16[2,4,128,256]{2,3,1,0:T(8,128)(2,1)S(1)}, bf16[2,4,128,256]{2,3,1,0:T(8,128)(2,1)S(1)}, u32[]{:S(2)}, u32[]{:S(2)}) collective-permute-start(bf16[2,4,128,256]{2,3,1,0:T(8,128)(2,1)S(1)} %get-tuple-element.496), channel_id=1, source_target_pairs={{64,0},{128,64},{192,128},{256,192},{320,256},{384,320},{448,384},... | collective-permute-start | bytes 1572872 | tf_op jit(solution)/shard_map/while/body/eval_jaxpr/ppermute | solution.py:35
  348.2 5.1 collective-permute-start.1
  350.1 19.9 %collective-permute-start.2 = (bf16[2,1,128,256]{2,3,1,0:T(8,128)(2,1)S(1)}, bf16[2,1,128,256]{2,3,1,0:T(8,128)(2,1)S(1)}, u32[]{:S(2)}, u32[]{:S(2)}) collective-permute-start(bf16[2,1,128,256]{2,3,1,0:T(8,128)(2,1)S(1)} %get-tuple-element.475), channel_id=1, source_target_pairs={{0,1},{1,2},{2,3},{3,4},{4,5},{5,6},{6,7},{7,8},{8,9},{9,10},{10,1... | collective-permute-start | bytes 393224 | tf_op jit(solution)/shard_map/while/body/eval_jaxpr/ppermute | solution.py:23
  370.9 8.5 %collective-permute-start.3 = (bf16[2,2,128,256]{2,3,1,0:T(8,128)(2,1)S(1)}, bf16[2,2,128,256]{2,3,1,0:T(8,128)(2,1)S(1)}, u32[]{:S(2)}, u32[]{:S(2)}) collective-permute-start(bf16[2,2,128,256]{2,3,1,0:T(8,128)(2,1)S(1)} %get-tuple-element.476), channel_id=1, source_target_pairs={{1,0},{2,1},{3,2},{4,3},{5,4},{6,5},{7,6},{8,7},{9,8},{10,9},{11,1... | collective-permute-start | bytes 786440 | tf_op jit(solution)/shard_map/while/body/eval_jaxpr/ppermute | solution.py:25
  372.9 23.3 %collective-permute-start.4 = (bf16[2,2,128,256]{2,3,1,0:T(8,128)(2,1)S(1)}, bf16[2,2,128,256]{2,3,1,0:T(8,128)(2,1)S(1)}, u32[]{:S(2)}, u32[]{:S(2)}) collective-permute-start(bf16[2,2,128,256]{2,3,1,0:T(8,128)(2,1)S(1)} %get-tuple-element.477), channel_id=1, source_target_pairs={{0,1},{1,2},{2,3},{3,4},{4,5},{5,6},{6,7},{7,8},{8,9},{9,10},{10,1... | collective-permute-start | bytes 786440 | tf_op jit(solution)/shard_map/while/body/eval_jaxpr/ppermute | solution.py:23
  401.0 11.1 %collective-permute-start = (bf16[2,4,128,256]{2,3,1,0:T(8,128)(2,1)S(1)}, bf16[2,4,128,256]{2,3,1,0:T(8,128)(2,1)S(1)}, u32[]{:S(2)}, u32[]{:S(2)}) collective-permute-start(bf16[2,4,128,256]{2,3,1,0:T(8,128)(2,1)S(1)} %get-tuple-element.496), channel_id=1, source_target_pairs={{64,0},{128,64},{192,128},{256,192},{320,256},{384,320},{448,384},... | collective-permute-start | bytes 1572872 | tf_op jit(solution)/shard_map/while/body/eval_jaxpr/ppermute | solution.py:35
  412.1 5.6 %collective-permute-start.1 = (bf16[2,1,128,256]{2,3,1,0:T(8,128)(2,1)S(1)}, bf16[2,1,128,256]{2,3,1,0:T(8,128)(2,1)S(1)}, u32[]{:S(2)}, u32[]{:S(2)}) collective-permute-start(bf16[2,1,128,256]{2,3,1,0:T(8,128)(2,1)S(1)} %get-tuple-element.474), channel_id=1, source_target_pairs={{1,0},{2,1},{3,2},{4,3},{5,4},{6,5},{7,6},{8,7},{9,8},{10,9},{11,1... | collective-permute-start | bytes 393224 | tf_op jit(solution)/shard_map/while/body/eval_jaxpr/ppermute | solution.py:25
  414.0 20.4 %collective-permute-start.2 = (bf16[2,1,128,256]{2,3,1,0:T(8,128)(2,1)S(1)}, bf16[2,1,128,256]{2,3,1,0:T(8,128)(2,1)S(1)}, u32[]{:S(2)}, u32[]{:S(2)}) collective-permute-start(bf16[2,1,128,256]{2,3,1,0:T(8,128)(2,1)S(1)} %get-tuple-element.475), channel_id=1, source_target_pairs={{0,1},{1,2},{2,3},{3,4},{4,5},{5,6},{6,7},{7,8},{8,9},{9,10},{10,1... | collective-permute-start | bytes 393224 | tf_op jit(solution)/shard_map/while/body/eval_jaxpr/ppermute | solution.py:23
  435.3 8.2 %collective-permute-start.3 = (bf16[2,2,128,256]{2,3,1,0:T(8,128)(2,1)S(1)}, bf16[2,2,128,256]{2,3,1,0:T(8,128)(2,1)S(1)}, u32[]{:S(2)}, u32[]{:S(2)}) collective-permute-start(bf16[2,2,128,256]{2,3,1,0:T(8,128)(2,1)S(1)} %get-tuple-element.476), channel_id=1, source_target_pairs={{1,0},{2,1},{3,2},{4,3},{5,4},{6,5},{7,6},{8,7},{9,8},{10,9},{11,1... | collective-permute-start | bytes 786440 | tf_op jit(solution)/shard_map/while/body/eval_jaxpr/ppermute | solution.py:25
  437.2 23.1 %collective-permute-start.4 = (bf16[2,2,128,256]{2,3,1,0:T(8,128)(2,1)S(1)}, bf16[2,2,128,256]{2,3,1,0:T(8,128)(2,1)S(1)}, u32[]{:S(2)}, u32[]{:S(2)}) collective-permute-start(bf16[2,2,128,256]{2,3,1,0:T(8,128)(2,1)S(1)} %get-tuple-element.477), channel_id=1, source_target_pairs={{0,1},{1,2},{2,3},{3,4},{4,5},{5,6},{6,7},{7,8},{8,9},{9,10},{10,1... | collective-permute-start | bytes 786440 | tf_op jit(solution)/shard_map/while/body/eval_jaxpr/ppermute | solution.py:23
  465.2 11.1 %collective-permute-start = (bf16[2,4,128,256]{2,3,1,0:T(8,128)(2,1)S(1)}, bf16[2,4,128,256]{2,3,1,0:T(8,128)(2,1)S(1)}, u32[]{:S(2)}, u32[]{:S(2)}) collective-permute-start(bf16[2,4,128,256]{2,3,1,0:T(8,128)(2,1)S(1)} %get-tuple-element.496), channel_id=1, source_target_pairs={{64,0},{128,64},{192,128},{256,192},{320,256},{384,320},{448,384},... | collective-permute-start | bytes 1572872 | tf_op jit(solution)/shard_map/while/body/eval_jaxpr/ppermute | solution.py:35
  476.2 5.3 %collective-permute-start.1 = (bf16[2,1,128,256]{2,3,1,0:T(8,128)(2,1)S(1)}, bf16[2,1,128,256]{2,3,1,0:T(8,128)(2,1)S(1)}, u32[]{:S(2)}, u32[]{:S(2)}) collective-permute-start(bf16[2,1,128,256]{2,3,1,0:T(8,128)(2,1)S(1)} %get-tuple-element.474), channel_id=1, source_target_pairs={{1,0},{2,1},{3,2},{4,3},{5,4},{6,5},{7,6},{8,7},{9,8},{10,9},{11,1... | collective-permute-start | bytes 393224 | tf_op jit(solution)/shard_map/while/body/eval_jaxpr/ppermute | solution.py:25
  478.2 20.2 %collective-permute-start.2 = (bf16[2,1,128,256]{2,3,1,0:T(8,128)(2,1)S(1)}, bf16[2,1,128,256]{2,3,1,0:T(8,128)(2,1)S(1)}, u32[]{:S(2)}, u32[]{:S(2)}) collective-permute-start(bf16[2,1,128,256]{2,3,1,0:T(8,128)(2,1)S(1)} %get-tuple-element.475), channel_id=1, source_target_pairs={{0,1},{1,2},{2,3},{3,4},{4,5},{5,6},{6,7},{7,8},{8,9},{9,10},{10,1... | collective-permute-start | bytes 393224 | tf_op jit(solution)/shard_map/while/body/eval_jaxpr/ppermute | solution.py:23
  499.2 8.4 %collective-permute-start.3 = (bf16[2,2,128,256]{2,3,1,0:T(8,128)(2,1)S(1)}, bf16[2,2,128,256]{2,3,1,0:T(8,128)(2,1)S(1)}, u32[]{:S(2)}, u32[]{:S(2)}) collective-permute-start(bf16[2,2,128,256]{2,3,1,0:T(8,128)(2,1)S(1)} %get-tuple-element.476), channel_id=1, source_target_pairs={{1,0},{2,1},{3,2},{4,3},{5,4},{6,5},{7,6},{8,7},{9,8},{10,9},{11,1... | collective-permute-start | bytes 786440 | tf_op jit(solution)/shard_map/while/body/eval_jaxpr/ppermute | solution.py:25
  501.2 23.2 %collective-permute-start.4 = (bf16[2,2,128,256]{2,3,1,0:T(8,128)(2,1)S(1)}, bf16[2,2,128,256]{2,3,1,0:T(8,128)(2,1)S(1)}, u32[]{:S(2)}, u32[]{:S(2)}) collective-permute-start(bf16[2,2,128,256]{2,3,1,0:T(8,128)(2,1)S(1)} %get-tuple-element.477), channel_id=1, source_target_pairs={{0,1},{1,2},{2,3},{3,4},{4,5},{5,6},{6,7},{7,8},{8,9},{9,10},{10,1... | collective-permute-start | bytes 786440 | tf_op jit(solution)/shard_map/while/body/eval_jaxpr/ppermute | solution.py:23
  529.2 2.0 copy-start.6
  (21 other events, 20.8 us)
where the time goes:
time: 533 us; the launch traced here: 531 us
  waiting for transfers between devices  378 us (71%)
  starting transfers between devices  97.9 us (18%)
  local copies, waits for them, and re-layouts  27.6 us (5%)
  matrix products  15.1 us (3%)
  other arithmetic  10.8 us (2%)
    ppermute x16, waiting for transfers between devices, with_halo(): lax.ppermute(tail, axis, [(i, (i + 1) % count) for i in range(ends)])  268 us
    ppermute x8, waiting for transfers between devices, shifted(): return lax.ppermute(array, axis, pairs)  69.5 us
    ppermute x16, waiting for transfers between devices, with_halo(): lax.ppermute(head, axis, [((i + 1) % count, i) for i in range(ends)])  40.3 us
    ppermute x16, starting transfers between devices, with_halo(): lax.ppermute(tail, axis, [(i, (i + 1) % count) for i in range(ends)])  38 us
    ppermute x16, starting transfers between devices, with_halo(): lax.ppermute(head, axis, [((i + 1) % count, i) for i in range(ends)])  37.5 us
    ppermute x8, starting transfers between devices, shifted(): return lax.ppermute(array, axis, pairs)  22.4 us
    dot_general x8, matrix products, factor_apply(): jnp.einsum('tkcij,dtkjr->cdtir', blocks, picked, preferred_element_type=j...  15.1 us
    while x56, local copies, waits for them, and re-layouts  12.8 us
  transfers between devices with their start and end apart: 40, of which 40 were waited for; matrix products, arithmetic and copies ran while one was open for 0% of the time, Pallas kernels for 0%

commit v1 on v0

v1 whole, which is shorter than its diff:
```python
import functools
import math

import jax
import jax.numpy as jnp
from jax import lax
from jax.experimental import pallas as pl
from jax.experimental.pallas import tpu as pltpu
from jax.sharding import PartitionSpec as P

PML_FACTOR = 0.55
LATERAL_WEIGHT = 0.25
CHUNK = 32
DEPTH = 1
NT = (((1,), (1,)), ((), ()))


def sweep_kernel(
    sweeps,
    tiles,
    idx_ref,
    thick_ref,
    src_hbm,
    fwd_hbm,
    fac_hbm,
    out_hbm,
    grad_ref,
    s_nat,
    f_nat,
    fac,
    s_t,
    gq,
    mats,
    vin,
    vout,
    onat,
    part,
    wext,
    hsend,
    hrecv,
    load_sem,
    zsend_sem,
    zrecv_sem,
    hsend_sem,
    hrecv_sem,
    out_sem,
):
    rows, rhs, wide = vin.shape
    block = wide // 2
    nonzero = mats.shape[1]
    chunks = rhs // CHUNK
    z = lax.axis_index("sweep")
    t = lax.axis_index("tile")
    has_left = t > 0
    has_right = t < tiles - 1
    has_above = z < sweeps - 1
    has_below = z > 0
    left = jnp.maximum(t - 1, 0)
    right = jnp.minimum(t + 1, tiles - 1)
    below = jnp.maximum(z - 1, 0)

    loads = [
        pltpu.make_async_copy(src_hbm, s_nat, load_sem.at[0]),
        pltpu.make_async_copy(fac_hbm, fac, load_sem.at[1]),
        pltpu.make_async_copy(fwd_hbm, f_nat, load_sem.at[2]),
    ]
    for copy in loads:
        copy.start()

    barrier = pltpu.get_barrier_semaphore()

    @pl.when(has_above)
    def _():
        pl.semaphore_signal(barrier, inc=1, device_id={"sweep": jnp.minimum(z + 1, sweeps - 1)})

    @pl.when(has_left)
    def _():
        pl.semaphore_signal(barrier, inc=1, device_id={"tile": left})

    @pl.when(has_right)
    def _():
        pl.semaphore_signal(barrier, inc=1, device_id={"tile": right})

    thick = thick_ref[...]
    in_pml = (z < thick) | (z >= sweeps - thick)
    gain = jnp.where(in_pml, PML_FACTOR * LATERAL_WEIGHT, LATERAL_WEIGHT).astype(jnp.float32)
    gq[...] = jnp.transpose(jnp.broadcast_to(gain, (block, rhs)), (1, 0))

    @pl.when(jnp.logical_not(has_above))
    def _():
        vin[...] = jnp.zeros_like(vin)

    @pl.when(jnp.logical_not(has_left))
    def _():
        hrecv[0] = jnp.zeros(hrecv.shape[1:], hrecv.dtype)

    @pl.when(jnp.logical_not(has_right))
    def _():
        hrecv[1] = jnp.zeros(hrecv.shape[1:], hrecv.dtype)

    loads[0].wait()

    def turn_source(x, carry):
        for c in range(2):
            s_t[x, :, c * block : (c + 1) * block] = jnp.transpose(s_nat[c, 0, x], (1, 0))
        return carry

    lax.fori_loop(0, rows, turn_source, 0)

    loads[1].wait()

    def build(x, carry):
        for k in range(nonzero):
            re = fac[0, x, k, 0]
            im = fac[0, x, k, 1]
            mats[x, k, :block, :block] = re
            mats[x, k, :block, block:] = -im
            mats[x, k, block:, :block] = im
            mats[x, k, block:, block:] = re
        return carry

    lax.fori_loop(0, rows, build, 0)

    pl.semaphore_wait(
        barrier,
        has_below.astype(jnp.int32) + has_left.astype(jnp.int32) + has_right.astype(jnp.int32),
    )

    lane = lax.broadcasted_iota(jnp.int32, (CHUNK, block), 1)
    left_on = has_left.astype(jnp.float32)
    right_on = has_right.astype(jnp.float32)

    def span(g):
        return pl.ds(pl.multiple_of(g * CHUNK, CHUNK), CHUNK)

    def hand_down(g):
        return pltpu.make_async_remote_copy(
            src_ref=vout.at[:, span(g)],
            dst_ref=vin.at[:, span(g)],
            send_sem=zsend_sem.at[g],
            recv_sem=zrecv_sem.at[g],
            device_id={"sweep": below},
        )

    def to_left(g):
        return pltpu.make_async_remote_copy(
            src_ref=hsend.at[0, :, span(g)],
            dst_ref=hrecv.at[1, :, span(g)],
            send_sem=hsend_sem.at[0, g],
            recv_sem=hrecv_sem.at[1, g],
            device_id={"tile": left},
        )

    def to_right(g):
        return pltpu.make_async_remote_copy(
            src_ref=hsend.at[1, :, span(g)],
            dst_ref=hrecv.at[0, :, span(g)],
            send_sem=hsend_sem.at[1, g],
            recv_sem=hrecv_sem.at[0, g],
            device_id={"tile": right},
        )

    def edges_out(g):
        rs = span(g)

        @pl.when(has_above)
        def _():
            hand_down(g).wait_recv()

        scale = gq[rs, :]
        for c in range(2):
            ls = slice(c * block, (c + 1) * block)
            v = [vin[x, rs, ls].astype(jnp.float32) for x in range(rows)]
            for x in range(rows):
                up = jnp.where(lane == block - 1, 0.0, pltpu.roll(v[x], block - 1, 1))
                down = jnp.where(lane == 0, 0.0, pltpu.roll(v[x], 1, 1))
                total = up + down
                if x > 0:
                    total = total + v[x - 1]
                if x < rows - 1:
                    total = total + v[x + 1]
                w = s_t[x, rs, ls].astype(jnp.float32) - scale * total
                low = w.astype(jnp.bfloat16)
                if x == 0:
                    part[0, rs, ls] = w
                    hsend[0, 1, rs, ls] = low
                    hsend[0, 0, rs, ls] = vin[0, rs, ls]
                elif x == rows - 1:
                    part[1, rs, ls] = w
                    hsend[1, 1, rs, ls] = low
                    hsend[1, 0, rs, ls] = vin[rows - 1, rs, ls]
                else:
                    wext[2 + x, rs, ls] = low
                    if x == 1:
                        hsend[0, 2, rs, ls] = low
                    if x == rows - 2:
                        hsend[1, 2, rs, ls] = low

        @pl.when(has_left)
        def _():
            to_left(g).start()

        @pl.when(has_right)
        def _():
            to_right(g).start()

    def rows_out(g):
        rs = span(g)

        @pl.when(has_left)
        def _():
            to_right(g).wait_recv()

        @pl.when(has_right)
        def _():
            to_left(g).wait_recv()

        scale = gq[rs, :]
        for c in range(2):
            ls = slice(c * block, (c + 1) * block)
            near = hrecv[0, 0, rs, ls].astype(jnp.float32)
            wext[2, rs, ls] = (part[0, rs, ls] - scale * near).astype(jnp.bfloat16)
            near = hrecv[1, 0, rs, ls].astype(jnp.float32)
            wext[rows + 1, rs, ls] = (part[1, rs, ls] - scale * near).astype(jnp.bfloat16)
            mine = vin[0, rs, ls].astype(jnp.float32) * left_on
            wext[1, rs, ls] = (hrecv[0, 1, rs, ls].astype(jnp.float32) - scale * mine).astype(
                jnp.bfloat16
            )
            mine = vin[rows - 1, rs, ls].astype(jnp.float32) * right_on
            wext[rows + 2, rs, ls] = (
                hrecv[1, 1, rs, ls].astype(jnp.float32) - scale * mine
            ).astype(jnp.bfloat16)
            wext[0, rs, ls] = hrecv[0, 2, rs, ls]
            wext[rows + 3, rs, ls] = hrecv[1, 2, rs, ls]
        for x in range(rows):
            acc = None
            for k in range(nonzero):
                term = lax.dot_general(
                    wext[idx_ref[x, k], rs, :],
                    mats[x, k],
                    NT,
                    preferred_element_type=jnp.float32,
                )
                acc = term if acc is None else acc + term
            vout[x, rs, :] = acc.astype(jnp.bfloat16)

        @pl.when(has_below)
        def _():
            hand_down(g).start()

    for g in range(DEPTH):
        edges_out(jnp.int32(g))

    def step(g, carry):
        @pl.when(g + DEPTH < chunks)
        def _():
            edges_out(g + DEPTH)

        rows_out(g)
        return carry

    lax.fori_loop(0, chunks, step, 0)

    loads[2].wait()

    norm_scale = 1.0 / math.sqrt(rhs)

    def finish(x, carry):
        total = jnp.zeros((block, block), jnp.float32)
        for c in range(2):
            for h in range(rhs // block):
                hs = slice(h * block, (h + 1) * block)
                turned = jnp.transpose(vout[x, hs, c * block : (c + 1) * block], (1, 0))
                onat[c, 0, x, :, hs] = turned
                total = total + f_nat[c, 0, x, :, hs].astype(jnp.float32) * turned.astype(
                    jnp.float32
                )
        turned = jnp.transpose(total, (1, 0))
        grad_ref[x] = jnp.sum(turned, axis=0, keepdims=True) * norm_scale
        return carry

    lax.fori_loop(0, rows, finish, 0)

    store = pltpu.make_async_copy(onat, out_hbm, out_sem)
    store.start()

    def drain(g, carry):
        @pl.when(has_below)
        def _():
            hand_down(g).wait_send()

        @pl.when(has_left)
        def _():
            to_left(g).wait_send()

        @pl.when(has_right)
        def _():
            to_right(g).wait_send()

        return carry

    lax.fori_loop(0, chunks, drain, 0)
    store.wait()


def on_device(sweeps, tiles, adjoint_source, forward_field, factor_blocks, factor_index, pml_thickness):
    _, layers, rows, block, rhs = adjoint_source.shape
    assert layers == 1
    nonzero = factor_blocks.shape[2]
    wide = 2 * block
    chunks = rhs // CHUNK
    bf16 = jnp.bfloat16
    f32 = jnp.float32
    any_spec = pl.BlockSpec(memory_space=pl.ANY)
    vmem_spec = pl.BlockSpec(memory_space=pltpu.VMEM)
    adjoint, gradient = pl.pallas_call(
        functools.partial(sweep_kernel, sweeps, tiles),
        out_shape=(
            jax.ShapeDtypeStruct(adjoint_source.shape, bf16),
            jax.ShapeDtypeStruct((rows, 1, block), f32),
        ),
        in_specs=[
            pl.BlockSpec(memory_space=pltpu.SMEM),
            vmem_spec,
            any_spec,
            any_spec,
            any_spec,
        ],
        out_specs=(any_spec, vmem_spec),
        scratch_shapes=[
            pltpu.VMEM(adjoint_source.shape, bf16),
            pltpu.VMEM(forward_field.shape, bf16),
            pltpu.VMEM(factor_blocks.shape, bf16),
            pltpu.VMEM((rows, rhs, wide), bf16),
            pltpu.VMEM((rhs, block), f32),
            pltpu.VMEM((rows, nonzero, wide, wide), bf16),
            pltpu.VMEM((rows, rhs, wide), bf16),
            pltpu.VMEM((rows, rhs, wide), bf16),
            pltpu.VMEM(adjoint_source.shape, bf16),
            pltpu.VMEM((2, rhs, wide), f32),
            pltpu.VMEM((rows + 4, rhs, wide), bf16),
            pltpu.VMEM((2, 3, rhs, wide), bf16),
            pltpu.VMEM((2, 3, rhs, wide), bf16),
            pltpu.SemaphoreType.DMA((3,)),
            pltpu.SemaphoreType.DMA((chunks,)),
            pltpu.SemaphoreType.DMA((chunks,)),
            pltpu.SemaphoreType.DMA((2, chunks)),
            pltpu.SemaphoreType.DMA((2, chunks)),
            pltpu.SemaphoreType.DMA,
        ],
        compiler_params=pltpu.CompilerParams(
            collective_id=0, has_side_effects=True, vmem_limit_bytes=40 * 1024 * 1024
        ),
    )(
        factor_index[0],
        pml_thickness[None],
        adjoint_source,
        forward_field,
        factor_blocks,
    )
    return adjoint, gradient.reshape(1, rows, block)


def solution(mesh):
    placed = (
        P(None, "sweep", "tile", None, None),
        P(None, "sweep", "tile", None, None),
        P("sweep", "tile", None, None, None, None),
        P("sweep", "tile", None),
        P(),
    )
    return jax.shard_map(
        functools.partial(on_device, mesh.shape["sweep"], mesh.shape["tile"]),
        mesh=mesh,
        in_specs=placed,
        out_specs=(P(None, "sweep", "tile", None, None), P("sweep", "tile", None)),
        check_vma=False,
    )
```

time: 533 us -> 159 us (0.30)
  the two profiles are of different devices: /device:TPU:448 before, /device:TPU:31 now
where the time goes in v1:
time: 159 us
  Pallas kernels  152 us (96%)
  local copies, waits for them, and re-layouts  6.03 us (4%)
    pallas_call x1, Pallas kernels, on_device(): pl.pallas_call(functools.partial(sweep_kernel, sweeps, tiles), out_shape=...  152 us
    unnamed x13, local copies, waits for them, and re-layouts  6.03 us

profile of v1, /device:TPU:31, one launch (start us, length us, event | category | flops | bytes accessed | tf_op | source)
XLA Modules:
  0.0 158.5 jit_solution(16999070513988098080)
XLA Ops:
  0.6 0.0 copy-start.4
  0.6 0.7 copy-done.4
  1.3 0.1 copy.7
  1.4 0.0 copy-start.3
  1.4 0.7 copy-done.3
  2.1 0.0 copy-start
  2.1 1.1 copy-done
  3.2 0.0 copy-start.1
  3.2 1.0 copy-done.1
  4.3 0.0 copy-start.2
  4.3 1.0 copy-done.2
  5.3 151.8 %shard_map.68 = (bf16[2,1,4,128,256]{4,3,2,1,0:T(8,128)(2,1)S(1)}, f32[4,1,128]{2,1,0:T(1,128)S(1)}) custom-call(s32[4,3]{1,0:T(4,128)S(1)} %bitcast.3, s32[1,256]{1,0:T(1,128)S(1)} %bitcast.5, bf16[2,1,4,128,256]{4,3,2,1,0:T(8,128)(2,1)S(1)} %copy-done.1, bf16[2,1,4,128,256]{4,3,2,1,0:T(8,128)(2,1)S(1)} %copy-done.2, ...), custom_call_target="tpu_custom_call" | custom-call | tf_op jit(solution)/shard_map/pallas_call | solution.py:316
  157.1 0.8 copy.10
  157.9 0.6 copy.11
Async XLA Ops:
  0.6 0.7 copy-start.4
  1.4 0.7 copy-start.3
  2.1 1.1 copy-start
  3.2 1.0 copy-start.1
  4.3 1.0 copy-start.2

commit v2 on v1

--- a/solution.py
+++ b/solution.py
@@ -11,39 +11,44 @@
 PML_FACTOR = 0.55
 LATERAL_WEIGHT = 0.25
 CHUNK = 32
-DEPTH = 1
+DEPTH = 2
 NT = (((1,), (1,)), ((), ()))
 
 
 def sweep_kernel(
     sweeps,
     tiles,
-    idx_ref,
-    thick_ref,
+    idx_hbm,
+    thick_hbm,
     src_hbm,
     fwd_hbm,
     fac_hbm,
-    out_hbm,
+    out_ref,
     grad_ref,
+    idx_ref,
+    thick_ref,
     s_nat,
     f_nat,
     fac,
     s_t,
+    s_next,
     gq,
+    gq_next,
     mats,
     vin,
     vout,
-    onat,
     part,
     wext,
     hsend,
+    fsend,
     hrecv,
     load_sem,
+    up_sem,
     zsend_sem,
     zrecv_sem,
     hsend_sem,
     hrecv_sem,
-    out_sem,
+    fsend_sem,
 ):
     rows, rhs, wide = vin.shape
     block = wide // 2
@@ -55,38 +60,50 @@
     has_right = t < tiles - 1
     has_above = z < sweeps - 1
     has_below = z > 0
+    top = jnp.logical_not(has_above)
+    far_left = t == tiles // 2
+    far_right = t == tiles // 2 - 1
+    is_far = far_left | far_right
+    send_left = has_left & (jnp.logical_not(far_left) | top)
+    send_right = has_right & (jnp.logical_not(far_right) | top)
     left = jnp.maximum(t - 1, 0)
     right = jnp.minimum(t + 1, tiles - 1)
     below = jnp.maximum(z - 1, 0)
+    above = jnp.minimum(z + 1, sweeps - 1)
+    partner = jnp.where(far_left, left, right)
+    partner_side = far_left.astype(jnp.int32)
 
     loads = [
         pltpu.make_async_copy(src_hbm, s_nat, load_sem.at[0]),
-        pltpu.make_async_copy(fac_hbm, fac, load_sem.at[1]),
-        pltpu.make_async_copy(fwd_hbm, f_nat, load_sem.at[2]),
+        pltpu.make_async_copy(thick_hbm, thick_ref, load_sem.at[1]),
+        pltpu.make_async_copy(idx_hbm, idx_ref, load_sem.at[2]),
+        pltpu.make_async_copy(fac_hbm, fac, load_sem.at[3]),
+        pltpu.make_async_copy(fwd_hbm, f_nat, load_sem.at[4]),
     ]
+
+    barrier = pltpu.get_barrier_semaphore()
+
+    def greet(wanted, **device_id):
+        @pl.when(wanted)
+        def _():
+            pl.semaphore_signal(barrier, inc=1, device_id=device_id)
+
+    greet(is_far & has_above, sweep=above, tile=partner)
+    greet(send_left, tile=left)
+    greet(send_right, tile=right)
+    greet(has_above, sweep=above)
+    greet(is_far & has_below, sweep=below)
+
     for copy in loads:
         copy.start()
 
-    barrier = pltpu.get_barrier_semaphore()
-
-    @pl.when(has_above)
-    def _():
-        pl.semaphore_signal(barrier, inc=1, device_id={"sweep": jnp.minimum(z + 1, sweeps - 1)})
-
-    @pl.when(has_left)
-    def _():
-        pl.semaphore_signal(barrier, inc=1, device_id={"tile": left})
-
-    @pl.when(has_right)
-    def _():
-        pl.semaphore_signal(barrier, inc=1, device_id={"tile": right})
-
-    thick = thick_ref[...]
-    in_pml = (z < thick) | (z >= sweeps - thick)
-    gain = jnp.where(in_pml, PML_FACTOR * LATERAL_WEIGHT, LATERAL_WEIGHT).astype(jnp.float32)
-    gq[...] = jnp.transpose(jnp.broadcast_to(gain, (block, rhs)), (1, 0))
-
-    @pl.when(jnp.logical_not(has_above))
+    def gain_rows(depth):
+        thick = thick_ref[...]
+        in_pml = (depth < thick) | (depth >= sweeps - thick)
+        gain = jnp.where(in_pml, PML_FACTOR * LATERAL_WEIGHT, LATERAL_WEIGHT).astype(jnp.float32)
+        return jnp.transpose(jnp.broadcast_to(gain, (block, rhs)), (1, 0))
+
+    @pl.when(top)
     def _():
         vin[...] = jnp.zeros_like(vin)
 
@@ -98,6 +115,8 @@
     def _():
         hrecv[1] = jnp.zeros(hrecv.shape[1:], hrecv.dtype)
 
+    loads[1].wait()
+    gq[...] = gain_rows(z)
     loads[0].wait()
 
     def turn_source(x, carry):
@@ -106,8 +125,6 @@
         return carry
 
     lax.fori_loop(0, rows, turn_source, 0)
-
-    loads[1].wait()
 
     def build(x, carry):
         for k in range(nonzero):
@@ -119,16 +136,32 @@
             mats[x, k, block:, block:] = re
         return carry
 
-    lax.fori_loop(0, rows, build, 0)
-
-    pl.semaphore_wait(
-        barrier,
-        has_below.astype(jnp.int32) + has_left.astype(jnp.int32) + has_right.astype(jnp.int32),
-    )
+    one = [
+        wanted.astype(jnp.int32)
+        for wanted in (has_below, send_left, send_right, is_far & has_below, is_far & has_above)
+    ]
+    pl.semaphore_wait(barrier, one[0] + one[1] + one[2] + one[3] + one[4])
 
     lane = lax.broadcasted_iota(jnp.int32, (CHUNK, block), 1)
     left_on = has_left.astype(jnp.float32)
     right_on = has_right.astype(jnp.float32)
+
+    def beside(v):
+        up = jnp.where(lane == block - 1, 0.0, pltpu.roll(v, block - 1, 1))
+        down = jnp.where(lane == 0, 0.0, pltpu.roll(v, 1, 1))
+        return up + down
+
+    hand_up = pltpu.make_async_remote_copy(
+        src_ref=s_t.at[pl.ds(jnp.where(far_left, 0, rows - 2), 2)],
+        dst_ref=s_next,
+        send_sem=up_sem.at[0],
+        recv_sem=up_sem.at[1],
+        device_id={"sweep": above},
+    )
+
+    @pl.when(is_far & has_above)
+    def _():
+        hand_up.start()
 
     def span(g):
         return pl.ds(pl.multiple_of(g * CHUNK, CHUNK), CHUNK)
@@ -160,6 +193,15 @@
             device_id={"tile": right},
         )
 
+    def to_partner(g):
+        return pltpu.make_async_remote_copy(
+            src_ref=fsend.at[:, span(g)],
+            dst_ref=hrecv.at[partner_side, :, span(g)],
+            send_sem=fsend_sem.at[g],
+            recv_sem=hrecv_sem.at[partner_side, g],
+            device_id={"sweep": below, "tile": partner},
+        )
+
     def edges_out(g):
         rs = span(g)
 
@@ -172,9 +214,7 @@
             ls = slice(c * block, (c + 1) * block)
             v = [vin[x, rs, ls].astype(jnp.float32) for x in range(rows)]
             for x in range(rows):
-                up = jnp.where(lane == block - 1, 0.0, pltpu.roll(v[x], block - 1, 1))
-                down = jnp.where(lane == 0, 0.0, pltpu.roll(v[x], 1, 1))
-                total = up + down
+                total = beside(v[x])
                 if x > 0:
                     total = total + v[x - 1]
                 if x < rows - 1:
@@ -196,11 +236,11 @@
                     if x == rows - 2:
                         hsend[1, 2, rs, ls] = low
 
-        @pl.when(has_left)
+        @pl.when(send_left)
         def _():
             to_left(g).start()
 
-        @pl.when(has_right)
+        @pl.when(send_right)
         def _():
             to_right(g).start()
 
@@ -232,36 +272,72 @@
             ).astype(jnp.bfloat16)
             wext[0, rs, ls] = hrecv[0, 2, rs, ls]
             wext[rows + 3, rs, ls] = hrecv[1, 2, rs, ls]
-        for x in range(rows):
+        for j in range(rows):
+            x = jnp.where(far_right, rows - 1 - j, j)
             acc = None
             for k in range(nonzero):
                 term = lax.dot_general(
-                    wext[idx_ref[x, k], rs, :],
+                    wext[idx_ref[k, 0, x], rs, :],
                     mats[x, k],
                     NT,
                     preferred_element_type=jnp.float32,
                 )
                 acc = term if acc is None else acc + term
             vout[x, rs, :] = acc.astype(jnp.bfloat16)
+            if j == rows - 2:
+                @pl.when(is_far & has_below)
+                def _():
+                    step_in = jnp.where(far_right, -1, 1)
+                    edge = jnp.where(far_right, rows - 1, 0)
+                    s_edge = jnp.where(far_right, 1, 0)
+                    scale = gq_next[rs, :]
+                    for c in range(2):
+                        ls = slice(c * block, (c + 1) * block)
+                        v0 = vout[edge, rs, ls].astype(jnp.float32)
+                        v1 = vout[edge + step_in, rs, ls].astype(jnp.float32)
+                        v2 = vout[edge + 2 * step_in, rs, ls].astype(jnp.float32)
+                        s0 = s_next[s_edge, rs, ls].astype(jnp.float32)
+                        s1 = s_next[1 - s_edge, rs, ls].astype(jnp.float32)
+                        fsend[0, rs, ls] = vout[edge, rs, ls]
+                        fsend[1, rs, ls] = (s0 - scale * (v1 + beside(v0))).astype(jnp.bfloat16)
+                        fsend[2, rs, ls] = (s1 - scale * (v0 + v2 + beside(v1))).astype(
+                            jnp.bfloat16
+                        )
+                    to_partner(g).start()
 
         @pl.when(has_below)
         def _():
             hand_down(g).start()
 
-    for g in range(DEPTH):
-        edges_out(jnp.int32(g))
+    def first_edges(g, carry):
+        edges_out(g)
+        return carry
+
+    ahead = jnp.where(top, chunks, DEPTH)
+    lax.fori_loop(0, jnp.where(top, chunks, 0), first_edges, 0)
+
+    loads[3].wait()
+    loads[2].wait()
+    lax.fori_loop(0, rows, build, 0)
+
+    @pl.when(is_far & has_below)
+    def _():
+        gq_next[...] = gain_rows(z - 1)
+        hand_up.wait_recv()
+
+    lax.fori_loop(0, jnp.where(top, 0, DEPTH), first_edges, 0)
 
     def step(g, carry):
-        @pl.when(g + DEPTH < chunks)
-        def _():
-            edges_out(g + DEPTH)
+        @pl.when(g + ahead < chunks)
+        def _():
+            edges_out(g + ahead)
 
         rows_out(g)
         return carry
 
     lax.fori_loop(0, chunks, step, 0)
 
-    loads[2].wait()
+    loads[4].wait()
 
     norm_scale = 1.0 / math.sqrt(rhs)
 
@@ -271,36 +347,40 @@
             for h in range(rhs // block):
                 hs = slice(h * block, (h + 1) * block)
                 turned = jnp.transpose(vout[x, hs, c * block : (c + 1) * block], (1, 0))
-                onat[c, 0, x, :, hs] = turned
+                out_ref[c, 0, x, :, hs] = turned
                 total = total + f_nat[c, 0, x, :, hs].astype(jnp.float32) * turned.astype(
                     jnp.float32
                 )
         turned = jnp.transpose(total, (1, 0))
-        grad_ref[x] = jnp.sum(turned, axis=0, keepdims=True) * norm_scale
+        grad_ref[0, pl.ds(x, 1), :] = jnp.sum(turned, axis=0, keepdims=True) * norm_scale
         return carry
 
     lax.fori_loop(0, rows, finish, 0)
 
-    store = pltpu.make_async_copy(onat, out_hbm, out_sem)
-    store.start()
+    @pl.when(is_far & has_above)
+    def _():
+        hand_up.wait_send()
 
     def drain(g, carry):
         @pl.when(has_below)
         def _():
             hand_down(g).wait_send()
 
-        @pl.when(has_left)
+        @pl.when(is_far & has_below)
+        def _():
+            to_partner(g).wait_send()
+
+        @pl.when(send_left)
         def _():
             to_left(g).wait_send()
 
-        @pl.when(has_right)
+        @pl.when(send_right)
         def _():
             to_right(g).wait_send()
 
         return carry
 
     lax.fori_loop(0, chunks, drain, 0)
-    store.wait()
 
 
 def on_device(sweeps, tiles, adjoint_source, forward_field, factor_blocks, factor_index, pml_thickness):
@@ -311,54 +391,49 @@
     chunks = rhs // CHUNK
     bf16 = jnp.bfloat16
     f32 = jnp.float32
-    any_spec = pl.BlockSpec(memory_space=pl.ANY)
+    hbm_spec = pl.BlockSpec(memory_space=pltpu.HBM)
     vmem_spec = pl.BlockSpec(memory_space=pltpu.VMEM)
+    index = jnp.transpose(factor_index, (2, 0, 1))
+    thickness = pml_thickness[None]
     adjoint, gradient = pl.pallas_call(
         functools.partial(sweep_kernel, sweeps, tiles),
         out_shape=(
             jax.ShapeDtypeStruct(adjoint_source.shape, bf16),
-            jax.ShapeDtypeStruct((rows, 1, block), f32),
+            jax.ShapeDtypeStruct((1, rows, block), f32),
         ),
-        in_specs=[
-            pl.BlockSpec(memory_space=pltpu.SMEM),
-            vmem_spec,
-            any_spec,
-            any_spec,
-            any_spec,
-        ],
-        out_specs=(any_spec, vmem_spec),
+        in_specs=[hbm_spec] * 5,
+        out_specs=(vmem_spec, vmem_spec),
         scratch_shapes=[
+            pltpu.SMEM(index.shape, jnp.int32),
+            pltpu.VMEM(thickness.shape, jnp.int32),
             pltpu.VMEM(adjoint_source.shape, bf16),
             pltpu.VMEM(forward_field.shape, bf16),
             pltpu.VMEM(factor_blocks.shape, bf16),
             pltpu.VMEM((rows, rhs, wide), bf16),
+            pltpu.VMEM((2, rhs, wide), bf16),
+            pltpu.VMEM((rhs, block), f32),
             pltpu.VMEM((rhs, block), f32),
             pltpu.VMEM((rows, nonzero, wide, wide), bf16),
             pltpu.VMEM((rows, rhs, wide), bf16),
             pltpu.VMEM((rows, rhs, wide), bf16),
-            pltpu.VMEM(adjoint_source.shape, bf16),
             pltpu.VMEM((2, rhs, wide), f32),
             pltpu.VMEM((rows + 4, rhs, wide), bf16),
             pltpu.VMEM((2, 3, rhs, wide), bf16),
+            pltpu.VMEM((3, rhs, wide), bf16),
             pltpu.VMEM((2, 3, rhs, wide), bf16),
-            pltpu.SemaphoreType.DMA((3,)),
+            pltpu.SemaphoreType.DMA((5,)),
+            pltpu.SemaphoreType.DMA((2,)),
             pltpu.SemaphoreType.DMA((chunks,)),
             pltpu.SemaphoreType.DMA((chunks,)),
             pltpu.SemaphoreType.DMA((2, chunks)),
             pltpu.SemaphoreType.DMA((2, chunks)),
-            pltpu.SemaphoreType.DMA,
+            pltpu.SemaphoreType.DMA((chunks,)),
         ],
         compiler_params=pltpu.CompilerParams(
-            collective_id=0, has_side_effects=True, vmem_limit_bytes=40 * 1024 * 1024
+            collective_id=0, has_side_effects=True, vmem_limit_bytes=63 * 1024 * 1024
         ),
-    )(
-        factor_index[0],
-        pml_thickness[None],
-        adjoint_source,
-        forward_field,
-        factor_blocks,
-    )
-    return adjoint, gradient.reshape(1, rows, block)
+    )(index, thickness, adjoint_source, forward_field, factor_blocks)
+    return adjoint, gradient
 
 
 def solution(mesh):

time: 159 us -> 102 us (0.64)
  Pallas kernels: 152 us -> 99 us
  local copies, waits for them, and re-layouts: 6.03 us -> 2.45 us
    pallas_call x1, Pallas kernels: 152 us -> 99 us  [on_device(): pl.pallas_call(functools.partial(sweep_kernel, sweeps, tiles), out_shape=...]
    unnamed x13 -> x4, local copies, waits for them, and re-layouts: 6.03 us -> 2.45 us
where the time goes in v2:
time: 102 us
  Pallas kernels  99 us (97%)
  local copies, waits for them, and re-layouts  2.45 us (2%)
    pallas_call x1, Pallas kernels, on_device(): pl.pallas_call(functools.partial(sweep_kernel, sweeps, tiles), out_shape=...  99 us
    unnamed x4, local copies, waits for them, and re-layouts  2.45 us

profile of v2, /device:TPU:31, one launch (start us, length us, event | category | flops | bytes accessed | tf_op | source)
XLA Modules:
  0.0 102.1 jit_solution(13645129968508843883)
XLA Ops:
  0.6 99.0 %shard_map.68 = (bf16[2,1,4,128,256]{4,3,2,1,0:T(8,128)(2,1)}, f32[1,4,128]{2,1,0:T(4,128)}) custom-call(s32[3,1,4]{2,1,0:T(1,128)} %bitcast.2, s32[1,256]{1,0:T(1,128)} %bitcast.3, bf16[2,1,4,128,256]{4,3,2,1,0:T(8,128)(2,1)} %src_hbm.1, bf16[2,1,4,128,256]{4,3,2,1,0:T(8,128)(2,1)} %fwd_hbm.1, bf16[1,4,3,2,128,128]{5,4,3,2,1,0:T(8,128)(2,1)} %fac_hbm.1), custom_call_target="tpu_custom_call" | custom-call | tf_op jit(solution)/shard_map/pallas_call | solution.py:398
  99.6 0.0 copy-start
  99.6 1.9 %copy.9 = bf16[2,1,4,128,256]{4,3,2,1,0:T(8,128)(2,1)} copy(bf16[2,1,4,128,256]{4,3,2,1,0:T(8,128)(2,1)} %get-tuple-element.4) | data formatting | bytes 1048576
  101.5 0.0 copy-done
  101.5 0.6 copy.10
Async XLA Ops:
  99.6 1.9 %copy-start = (f32[1,4,128]{2,1,0:T(4,128)S(1)}, f32[1,4,128]{2,1,0:T(4,128)}, u32[]{:S(2)}) copy-start(f32[1,4,128]{2,1,0:T(4,128)} %get-tuple-element.5) | copy-start | bytes 6148

commit v3 on v2

--- a/solution.py
+++ b/solution.py
@@ -12,7 +12,7 @@
 LATERAL_WEIGHT = 0.25
 CHUNK = 32
 DEPTH = 2
-NT = (((1,), (1,)), ((), ()))
+FAR_EVERY = 8
 
 
 def sweep_kernel(
@@ -21,14 +21,16 @@
     idx_hbm,
     thick_hbm,
     src_hbm,
+    fac_hbm,
     fwd_hbm,
-    fac_hbm,
-    out_ref,
-    grad_ref,
+    out_hbm,
+    grad_hbm,
     idx_ref,
     thick_ref,
     s_nat,
     f_nat,
+    o_nat,
+    grad,
     fac,
     s_t,
     s_next,
@@ -49,6 +51,10 @@
     hsend_sem,
     hrecv_sem,
     fsend_sem,
+    frecv_sem,
+    out_sem,
+    passing,
+    leg_sem,
 ):
     rows, rhs, wide = vin.shape
     block = wide // 2
@@ -61,11 +67,15 @@
     has_above = z < sweeps - 1
     has_below = z > 0
     top = jnp.logical_not(has_above)
-    far_left = t == tiles // 2
-    far_right = t == tiles // 2 - 1
+    far_left = has_left & (lax.rem(t, FAR_EVERY) == 0)
+    far_right = has_right & (lax.rem(t, FAR_EVERY) == FAR_EVERY - 1)
     is_far = far_left | far_right
-    send_left = has_left & (jnp.logical_not(far_left) | top)
-    send_right = has_right & (jnp.logical_not(far_right) | top)
+    is_a = t == tiles // 2 - 1
+    is_b = t == tiles // 2
+    is_pair = is_a | is_b
+    via = (is_pair & top, ((t == 0) | (t == tiles - 1)) & top)
+    send_left = has_left & (jnp.logical_not(far_left) | (top & jnp.logical_not(is_b)))
+    send_right = has_right & (jnp.logical_not(far_right) | (top & jnp.logical_not(is_a)))
     left = jnp.maximum(t - 1, 0)
     right = jnp.minimum(t + 1, tiles - 1)
     below = jnp.maximum(z - 1, 0)
@@ -88,7 +98,11 @@
         def _():
             pl.semaphore_signal(barrier, inc=1, device_id=device_id)
 
-    greet(is_far & has_above, sweep=above, tile=partner)
+    greet(is_far & has_above & jnp.logical_not(is_pair & (z == sweeps - 2)), sweep=above, tile=partner)
+    between = jnp.where(is_a, 0, tiles - 1)
+    beyond = jnp.where(t == 0, tiles // 2, tiles // 2 - 1)
+    greet(via[1], tile=jnp.where(t == 0, tiles // 2 - 1, tiles // 2))
+    greet(via[0], tile=jnp.where(is_a, tiles - 1, 0))
     greet(send_left, tile=left)
     greet(send_right, tile=right)
     greet(has_above, sweep=above)
@@ -107,6 +121,10 @@
     def _():
         vin[...] = jnp.zeros_like(vin)
 
+    @pl.when(via[0])
+    def _():
+        hrecv[jnp.where(is_a, 1, 0), 0] = jnp.zeros(hrecv.shape[2:], hrecv.dtype)
+
     @pl.when(jnp.logical_not(has_left))
     def _():
         hrecv[0] = jnp.zeros(hrecv.shape[1:], hrecv.dtype)
@@ -130,17 +148,27 @@
         for k in range(nonzero):
             re = fac[0, x, k, 0]
             im = fac[0, x, k, 1]
+            re = jnp.transpose(re, (1, 0))
+            im = jnp.transpose(im, (1, 0))
             mats[x, k, :block, :block] = re
-            mats[x, k, :block, block:] = -im
-            mats[x, k, block:, :block] = im
+            mats[x, k, :block, block:] = im
+            mats[x, k, block:, :block] = -im
             mats[x, k, block:, block:] = re
         return carry
 
     one = [
         wanted.astype(jnp.int32)
-        for wanted in (has_below, send_left, send_right, is_far & has_below, is_far & has_above)
+        for wanted in (
+            has_below,
+            send_left,
+            send_right,
+            is_far & has_below & jnp.logical_not(via[0]),
+            is_far & has_above,
+            via[0],
+            via[1],
+        )
     ]
-    pl.semaphore_wait(barrier, one[0] + one[1] + one[2] + one[3] + one[4])
+    pl.semaphore_wait(barrier, sum(one[1:], one[0]))
 
     lane = lax.broadcasted_iota(jnp.int32, (CHUNK, block), 1)
     left_on = has_left.astype(jnp.float32)
@@ -198,9 +226,59 @@
             src_ref=fsend.at[:, span(g)],
             dst_ref=hrecv.at[partner_side, :, span(g)],
             send_sem=fsend_sem.at[g],
-            recv_sem=hrecv_sem.at[partner_side, g],
+            recv_sem=frecv_sem.at[g],
             device_id={"sweep": below, "tile": partner},
         )
+
+    def first_leg(g):
+        return pltpu.make_async_remote_copy(
+            src_ref=hsend.at[jnp.where(is_a, 1, 0), pl.ds(1, 2), span(g)],
+            dst_ref=passing.at[:, span(g)],
+            send_sem=leg_sem.at[0, g],
+            recv_sem=leg_sem.at[1, g],
+            device_id={"tile": between},
+        )
+
+    def second_leg(g):
+        return pltpu.make_async_remote_copy(
+            src_ref=passing.at[:, span(g)],
+            dst_ref=hrecv.at[jnp.where(t == 0, 0, 1), pl.ds(1, 2), span(g)],
+            send_sem=leg_sem.at[2, g],
+            recv_sem=leg_sem.at[3, g],
+            device_id={"tile": beyond},
+        )
+
+    def turned_half(h):
+        return slice(h * block, (h + 1) * block)
+
+    def keep(h):
+        return pltpu.make_async_copy(
+            o_nat.at[:, :, :, :, turned_half(h)],
+            out_hbm.at[:, :, :, :, turned_half(h)],
+            out_sem.at[h],
+        )
+
+    def finish(h):
+        hs = turned_half(h)
+
+        def one_row(x, carry):
+            total = jnp.zeros((block, block), jnp.float32)
+            for c in range(2):
+                turned = jnp.transpose(vout[x, hs, c * block : (c + 1) * block], (1, 0))
+                o_nat[c, 0, x, :, hs] = turned
+                total = total + f_nat[c, 0, x, :, hs].astype(jnp.float32) * turned.astype(
+                    jnp.float32
+                )
+            summed = jnp.sum(jnp.transpose(total, (1, 0)), axis=0, keepdims=True)
+            if h > 0:
+                summed = summed + grad[0, pl.ds(x, 1), :]
+            if h == rhs // block - 1:
+                summed = summed * (1.0 / math.sqrt(rhs))
+            grad[0, pl.ds(x, 1), :] = summed
+            return carry
+
+        lax.fori_loop(0, rows, one_row, 0)
+        keep(h).start()
 
     def edges_out(g):
         rs = span(g)
@@ -244,66 +322,94 @@
         def _():
             to_right(g).start()
 
+        @pl.when(via[0])
+        def _():
+            first_leg(g).start()
+
     def rows_out(g):
         rs = span(g)
 
-        @pl.when(has_left)
+        @pl.when(send_left)
         def _():
             to_right(g).wait_recv()
 
-        @pl.when(has_right)
+        @pl.when(send_right)
         def _():
             to_left(g).wait_recv()
 
-        scale = gq[rs, :]
-        for c in range(2):
-            ls = slice(c * block, (c + 1) * block)
-            near = hrecv[0, 0, rs, ls].astype(jnp.float32)
-            wext[2, rs, ls] = (part[0, rs, ls] - scale * near).astype(jnp.bfloat16)
-            near = hrecv[1, 0, rs, ls].astype(jnp.float32)
-            wext[rows + 1, rs, ls] = (part[1, rs, ls] - scale * near).astype(jnp.bfloat16)
-            mine = vin[0, rs, ls].astype(jnp.float32) * left_on
-            wext[1, rs, ls] = (hrecv[0, 1, rs, ls].astype(jnp.float32) - scale * mine).astype(
-                jnp.bfloat16
-            )
-            mine = vin[rows - 1, rs, ls].astype(jnp.float32) * right_on
-            wext[rows + 2, rs, ls] = (
-                hrecv[1, 1, rs, ls].astype(jnp.float32) - scale * mine
-            ).astype(jnp.bfloat16)
-            wext[0, rs, ls] = hrecv[0, 2, rs, ls]
-            wext[rows + 3, rs, ls] = hrecv[1, 2, rs, ls]
-        for j in range(rows):
-            x = jnp.where(far_right, rows - 1 - j, j)
+        @pl.when(is_far & has_above)
+        def _():
+            to_partner(g).wait_recv()
+
+        @pl.when(via[0])
+        def _():
+            second_leg(g).wait_recv()
+
+        def settle():
+            scale = gq[rs, :]
+            for c in range(2):
+                ls = slice(c * block, (c + 1) * block)
+                near = hrecv[0, 0, rs, ls].astype(jnp.float32)
+                wext[2, rs, ls] = (part[0, rs, ls] - scale * near).astype(jnp.bfloat16)
+                near = hrecv[1, 0, rs, ls].astype(jnp.float32)
+                wext[rows + 1, rs, ls] = (part[1, rs, ls] - scale * near).astype(jnp.bfloat16)
+                mine = vin[0, rs, ls].astype(jnp.float32) * left_on
+                wext[1, rs, ls] = (hrecv[0, 1, rs, ls].astype(jnp.float32) - scale * mine).astype(
+                    jnp.bfloat16
+                )
+                mine = vin[rows - 1, rs, ls].astype(jnp.float32) * right_on
+                wext[rows + 2, rs, ls] = (
+                    hrecv[1, 1, rs, ls].astype(jnp.float32) - scale * mine
+                ).astype(jnp.bfloat16)
+                wext[0, rs, ls] = hrecv[0, 2, rs, ls]
+                wext[rows + 3, rs, ls] = hrecv[1, 2, rs, ls]
+
+        def field_row(x):
             acc = None
             for k in range(nonzero):
-                term = lax.dot_general(
+                term = jnp.dot(
                     wext[idx_ref[k, 0, x], rs, :],
                     mats[x, k],
-                    NT,
                     preferred_element_type=jnp.float32,
                 )
                 acc = term if acc is None else acc + term
-            vout[x, rs, :] = acc.astype(jnp.bfloat16)
-            if j == rows - 2:
-                @pl.when(is_far & has_below)
-                def _():
-                    step_in = jnp.where(far_right, -1, 1)
-                    edge = jnp.where(far_right, rows - 1, 0)
-                    s_edge = jnp.where(far_right, 1, 0)
-                    scale = gq_next[rs, :]
-                    for c in range(2):
-                        ls = slice(c * block, (c + 1) * block)
-                        v0 = vout[edge, rs, ls].astype(jnp.float32)
-                        v1 = vout[edge + step_in, rs, ls].astype(jnp.float32)
-                        v2 = vout[edge + 2 * step_in, rs, ls].astype(jnp.float32)
-                        s0 = s_next[s_edge, rs, ls].astype(jnp.float32)
-                        s1 = s_next[1 - s_edge, rs, ls].astype(jnp.float32)
-                        fsend[0, rs, ls] = vout[edge, rs, ls]
-                        fsend[1, rs, ls] = (s0 - scale * (v1 + beside(v0))).astype(jnp.bfloat16)
-                        fsend[2, rs, ls] = (s1 - scale * (v0 + v2 + beside(v1))).astype(
-                            jnp.bfloat16
-                        )
-                    to_partner(g).start()
+            row = acc.astype(jnp.bfloat16)
+            vout[x, rs, :] = row
+            return row
+
+        def near_only():
+            settle()
+            for x in range(rows):
+                field_row(x)
+
+        def with_far(edge, inward):
+            settle()
+            v = [field_row(edge + i * inward) for i in range(3)]
+            scale = gq_next[rs, :]
+            first = 0 if inward > 0 else 1
+            fsend[0, rs, :] = v[0]
+            for c in range(2):
+                ls = slice(c * block, (c + 1) * block)
+                v0, v1, v2 = (row[:, ls].astype(jnp.float32) for row in v)
+                source = s_next[first, rs, ls].astype(jnp.float32)
+                fsend[1, rs, ls] = (source - scale * (v1 + beside(v0))).astype(jnp.bfloat16)
+                source = s_next[1 - first, rs, ls].astype(jnp.float32)
+                fsend[2, rs, ls] = (source - scale * (v0 + v2 + beside(v1))).astype(jnp.bfloat16)
+            to_partner(g).start()
+            for i in range(3, rows):
+                field_row(edge + i * inward)
+
+        @pl.when(far_left & has_below)
+        def _():
+            with_far(0, 1)
+
+        @pl.when(far_right & has_below)
+        def _():
+            with_far(rows - 1, -1)
+
+        @pl.when(jnp.logical_not(is_far & has_below))
+        def _():
+            near_only()
 
         @pl.when(has_below)
         def _():
@@ -313,8 +419,18 @@
         edges_out(g)
         return carry
 
-    ahead = jnp.where(top, chunks, DEPTH)
+    depth = jnp.where(is_far & (t != tiles // 2) & (t != tiles // 2 - 1), 1, DEPTH)
+    ahead = jnp.where(top, chunks, depth)
     lax.fori_loop(0, jnp.where(top, chunks, 0), first_edges, 0)
+
+    @pl.when(via[1])
+    def _():
+        def forward(g, carry):
+            first_leg(g).wait_recv()
+            second_leg(g).start()
+            return carry
+
+        lax.fori_loop(0, chunks, forward, 0)
 
     loads[3].wait()
     loads[2].wait()
@@ -325,7 +441,7 @@
         gq_next[...] = gain_rows(z - 1)
         hand_up.wait_recv()
 
-    lax.fori_loop(0, jnp.where(top, 0, DEPTH), first_edges, 0)
+    lax.fori_loop(0, jnp.where(top, 0, depth), first_edges, 0)
 
     def step(g, carry):
         @pl.when(g + ahead < chunks)
@@ -335,27 +451,28 @@
         rows_out(g)
         return carry
 
-    lax.fori_loop(0, chunks, step, 0)
-
-    loads[4].wait()
-
-    norm_scale = 1.0 / math.sqrt(rhs)
-
-    def finish(x, carry):
-        total = jnp.zeros((block, block), jnp.float32)
-        for c in range(2):
-            for h in range(rhs // block):
-                hs = slice(h * block, (h + 1) * block)
-                turned = jnp.transpose(vout[x, hs, c * block : (c + 1) * block], (1, 0))
-                out_ref[c, 0, x, :, hs] = turned
-                total = total + f_nat[c, 0, x, :, hs].astype(jnp.float32) * turned.astype(
-                    jnp.float32
-                )
-        turned = jnp.transpose(total, (1, 0))
-        grad_ref[0, pl.ds(x, 1), :] = jnp.sum(turned, axis=0, keepdims=True) * norm_scale
-        return carry
-
-    lax.fori_loop(0, rows, finish, 0)
+    halves = rhs // block
+    per_half = chunks // halves
+    for h in range(halves - 1):
+        lax.fori_loop(h * per_half, (h + 1) * per_half, step, 0)
+
+        @pl.when(jnp.logical_not(has_below))
+        def _():
+            loads[4].wait()
+            finish(h)
+
+    lax.fori_loop((halves - 1) * per_half, chunks, step, 0)
+
+    @pl.when(has_below)
+    def _():
+        loads[4].wait()
+        for h in range(halves - 1):
+            finish(h)
+
+    finish(halves - 1)
+    grad_copy = pltpu.make_async_copy(grad, grad_hbm, out_sem.at[halves])
+    grad_copy.start()
+
 
     @pl.when(is_far & has_above)
     def _():
@@ -378,9 +495,43 @@
         def _():
             to_right(g).wait_send()
 
+        @pl.when(via[0])
+        def _():
+            first_leg(g).wait_send()
+
+        @pl.when(via[1])
+        def _():
+            second_leg(g).wait_send()
+
         return carry
 
     lax.fori_loop(0, chunks, drain, 0)
+    for h in range(halves):
+        keep(h).wait()
+    grad_copy.wait()
+
+
+def copy_kernel(adjoint_in, gradient_in, adjoint_out, gradient_out, held, held_gradient, sem):
+    rows = adjoint_in.shape[2]
+    pieces = [(gradient_in, held_gradient, gradient_out)]
+    for c in range(2):
+        for x in range(rows):
+            pieces.append((adjoint_in.at[c, 0, x], held.at[c, x], adjoint_out.at[c, 0, x]))
+    fetched = [
+        pltpu.make_async_copy(source, here, sem.at[0, i])
+        for i, (source, here, _) in enumerate(pieces)
+    ]
+    stored = [
+        pltpu.make_async_copy(here, target, sem.at[1, i])
+        for i, (_, here, target) in enumerate(pieces)
+    ]
+    for copy in fetched:
+        copy.start()
+    for fetch, store in zip(fetched, stored):
+        fetch.wait()
+        store.start()
+    for copy in stored:
+        copy.wait()
 
 
 def on_device(sweeps, tiles, adjoint_source, forward_field, factor_blocks, factor_index, pml_thickness):
@@ -392,22 +543,24 @@
     bf16 = jnp.bfloat16
     f32 = jnp.float32
     hbm_spec = pl.BlockSpec(memory_space=pltpu.HBM)
-    vmem_spec = pl.BlockSpec(memory_space=pltpu.VMEM)
     index = jnp.transpose(factor_index, (2, 0, 1))
     thickness = pml_thickness[None]
-    adjoint, gradient = pl.pallas_call(
+    outs = (
+        jax.ShapeDtypeStruct(adjoint_source.shape, bf16),
+        jax.ShapeDtypeStruct((1, rows, block), f32),
+    )
+    fields = pl.pallas_call(
         functools.partial(sweep_kernel, sweeps, tiles),
-        out_shape=(
-            jax.ShapeDtypeStruct(adjoint_source.shape, bf16),
-            jax.ShapeDtypeStruct((1, rows, block), f32),
-        ),
+        out_shape=outs,
         in_specs=[hbm_spec] * 5,
-        out_specs=(vmem_spec, vmem_spec),
+        out_specs=(hbm_spec, hbm_spec),
         scratch_shapes=[
             pltpu.SMEM(index.shape, jnp.int32),
             pltpu.VMEM(thickness.shape, jnp.int32),
             pltpu.VMEM(adjoint_source.shape, bf16),
             pltpu.VMEM(forward_field.shape, bf16),
+            pltpu.VMEM(adjoint_source.shape, bf16),
+            pltpu.VMEM((1, rows, block), f32),
             pltpu.VMEM(factor_blocks.shape, bf16),
             pltpu.VMEM((rows, rhs, wide), bf16),
             pltpu.VMEM((2, rhs, wide), bf16),
@@ -428,12 +581,26 @@
             pltpu.SemaphoreType.DMA((2, chunks)),
             pltpu.SemaphoreType.DMA((2, chunks)),
             pltpu.SemaphoreType.DMA((chunks,)),
+            pltpu.SemaphoreType.DMA((chunks,)),
+            pltpu.SemaphoreType.DMA((rhs // block + 1,)),
+            pltpu.VMEM((2, rhs, wide), bf16),
+            pltpu.SemaphoreType.DMA((4, chunks)),
         ],
         compiler_params=pltpu.CompilerParams(
             collective_id=0, has_side_effects=True, vmem_limit_bytes=63 * 1024 * 1024
         ),
-    )(index, thickness, adjoint_source, forward_field, factor_blocks)
-    return adjoint, gradient
+    )(index, thickness, adjoint_source, factor_blocks, forward_field)
+    return pl.pallas_call(
+        copy_kernel,
+        out_shape=outs,
+        in_specs=[hbm_spec] * 2,
+        out_specs=(hbm_spec, hbm_spec),
+        scratch_shapes=[
+            pltpu.VMEM((2, rows, block, rhs), bf16),
+            pltpu.VMEM((1, rows, block), f32),
+            pltpu.SemaphoreType.DMA((2, 2 * rows + 1)),
+        ],
+    )(*fields)
 
 
 def solution(mesh):

time: 102 us -> 96 us (0.941)
  Pallas kernels: 99 us -> 95.2 us
  local copies, waits for them, and re-layouts: 2.45 us -> 0 us
    pallas_call x1, Pallas kernels: 99 us -> 93.3 us  [on_device(): pl.pallas_call(functools.partial(sweep_kernel, sweeps, tiles), out_shape=...]
    unnamed x4 -> x0, local copies, waits for them, and re-layouts: 2.45 us -> none
    pallas_call x0 -> x1, Pallas kernels: none -> 1.85 us  [on_device(): pl.pallas_call(copy_kernel, out_shape=outs, in_specs=[hbm_spec] * 2, out_...]
where the time goes in v3:
time: 96 us; the launch traced here: 95.8 us
  Pallas kernels  95.2 us (99%)
    pallas_call x1, Pallas kernels, on_device(): pl.pallas_call(functools.partial(sweep_kernel, sweeps, tiles), out_shape=...  93.3 us

profile of v3, /device:TPU:31, one launch (start us, length us, event | category | flops | bytes accessed | tf_op | source)
XLA Modules:
  0.0 95.8 jit_solution(103222643232188469)
XLA Ops:
  0.6 93.3 %shard_map.68 = (bf16[2,1,4,128,256]{4,3,2,1,0:T(8,128)(2,1)}, f32[1,4,128]{2,1,0:T(4,128)}) custom-call(s32[3,1,4]{2,1,0:T(1,128)} %bitcast.2, s32[1,256]{1,0:T(1,128)} %bitcast.3, bf16[2,1,4,128,256]{4,3,2,1,0:T(8,128)(2,1)} %src_hbm.1, bf16[1,4,3,2,128,128]{5,4,3,2,1,0:T(8,128)(2,1)} %fac_hbm.1, bf16[2,1,4,128,256]{4,3,2,1,0:T(8,128)(2,1)} %fwd_hbm.1), custom_call_target="tpu_custom_call" | custom-call | tf_op jit(solution)/shard_map/pallas_call | solution.py:552
  94.0 1.9 %shard_map.69 = (bf16[2,1,4,128,256]{4,3,2,1,0:T(8,128)(2,1)}, f32[1,4,128]{2,1,0:T(4,128)}) custom-call(bf16[2,1,4,128,256]{4,3,2,1,0:T(8,128)(2,1)} %get-tuple-element.4.adjoint_in, f32[1,4,128]{2,1,0:T(4,128)} %get-tuple-element.5.gradient_in), custom_call_target="tpu_custom_call" | custom-call | tf_op jit(solution)/shard_map/pallas_call | solution.py:593

commit v4 on v3

--- a/solution.py
+++ b/solution.py
@@ -23,14 +23,12 @@
     src_hbm,
     fac_hbm,
     fwd_hbm,
-    out_hbm,
-    grad_hbm,
+    o_nat,
+    grad,
     idx_ref,
     thick_ref,
     s_nat,
     f_nat,
-    o_nat,
-    grad,
     fac,
     s_t,
     s_next,
@@ -52,14 +50,13 @@
     hrecv_sem,
     fsend_sem,
     frecv_sem,
-    out_sem,
     passing,
     leg_sem,
 ):
-    rows, rhs, wide = vin.shape
+    chunks, rows, _, wide = vin.shape
+    rhs = chunks * CHUNK
     block = wide // 2
     nonzero = mats.shape[1]
-    chunks = rhs // CHUNK
     z = lax.axis_index("sweep")
     t = lax.axis_index("tile")
     has_left = t > 0
@@ -123,15 +120,15 @@
 
     @pl.when(via[0])
     def _():
-        hrecv[jnp.where(is_a, 1, 0), 0] = jnp.zeros(hrecv.shape[2:], hrecv.dtype)
+        hrecv[:, jnp.where(is_a, 1, 0), 0] = jnp.zeros((chunks,) + hrecv.shape[3:], hrecv.dtype)
 
     @pl.when(jnp.logical_not(has_left))
     def _():
-        hrecv[0] = jnp.zeros(hrecv.shape[1:], hrecv.dtype)
+        hrecv[:, 0] = jnp.zeros((chunks,) + hrecv.shape[2:], hrecv.dtype)
 
     @pl.when(jnp.logical_not(has_right))
     def _():
-        hrecv[1] = jnp.zeros(hrecv.shape[1:], hrecv.dtype)
+        hrecv[:, 1] = jnp.zeros((chunks,) + hrecv.shape[2:], hrecv.dtype)
 
     loads[1].wait()
     gq[...] = gain_rows(z)
@@ -196,8 +193,8 @@
 
     def hand_down(g):
         return pltpu.make_async_remote_copy(
-            src_ref=vout.at[:, span(g)],
-            dst_ref=vin.at[:, span(g)],
+            src_ref=vout.at[g],
+            dst_ref=vin.at[g],
             send_sem=zsend_sem.at[g],
             recv_sem=zrecv_sem.at[g],
             device_id={"sweep": below},
@@ -205,8 +202,8 @@
 
     def to_left(g):
         return pltpu.make_async_remote_copy(
-            src_ref=hsend.at[0, :, span(g)],
-            dst_ref=hrecv.at[1, :, span(g)],
+            src_ref=hsend.at[g, 0],
+            dst_ref=hrecv.at[g, 1],
             send_sem=hsend_sem.at[0, g],
             recv_sem=hrecv_sem.at[1, g],
             device_id={"tile": left},
@@ -214,8 +211,8 @@
 
     def to_right(g):
         return pltpu.make_async_remote_copy(
-            src_ref=hsend.at[1, :, span(g)],
-            dst_ref=hrecv.at[0, :, span(g)],
+            src_ref=hsend.at[g, 1],
+            dst_ref=hrecv.at[g, 0],
             send_sem=hsend_sem.at[1, g],
             recv_sem=hrecv_sem.at[0, g],
             device_id={"tile": right},
@@ -223,8 +220,8 @@
 
     def to_partner(g):
         return pltpu.make_async_remote_copy(
-            src_ref=fsend.at[:, span(g)],
-            dst_ref=hrecv.at[partner_side, :, span(g)],
+            src_ref=fsend.at[g],
+            dst_ref=hrecv.at[g, partner_side],
             send_sem=fsend_sem.at[g],
             recv_sem=frecv_sem.at[g],
             device_id={"sweep": below, "tile": partner},
@@ -232,8 +229,8 @@
 
     def first_leg(g):
         return pltpu.make_async_remote_copy(
-            src_ref=hsend.at[jnp.where(is_a, 1, 0), pl.ds(1, 2), span(g)],
-            dst_ref=passing.at[:, span(g)],
+            src_ref=hsend.at[g, jnp.where(is_a, 1, 0), pl.ds(1, 2)],
+            dst_ref=passing.at[g],
             send_sem=leg_sem.at[0, g],
             recv_sem=leg_sem.at[1, g],
             device_id={"tile": between},
@@ -241,8 +238,8 @@
 
     def second_leg(g):
         return pltpu.make_async_remote_copy(
-            src_ref=passing.at[:, span(g)],
-            dst_ref=hrecv.at[jnp.where(t == 0, 0, 1), pl.ds(1, 2), span(g)],
+            src_ref=passing.at[g],
+            dst_ref=hrecv.at[g, jnp.where(t == 0, 0, 1), pl.ds(1, 2)],
             send_sem=leg_sem.at[2, g],
             recv_sem=leg_sem.at[3, g],
             device_id={"tile": beyond},
@@ -251,20 +248,15 @@
     def turned_half(h):
         return slice(h * block, (h + 1) * block)
 
-    def keep(h):
-        return pltpu.make_async_copy(
-            o_nat.at[:, :, :, :, turned_half(h)],
-            out_hbm.at[:, :, :, :, turned_half(h)],
-            out_sem.at[h],
-        )
-
     def finish(h):
         hs = turned_half(h)
 
         def one_row(x, carry):
             total = jnp.zeros((block, block), jnp.float32)
             for c in range(2):
-                turned = jnp.transpose(vout[x, hs, c * block : (c + 1) * block], (1, 0))
+                first = h * (block // CHUNK)
+                field = vout[first : first + block // CHUNK, x, :, c * block : (c + 1) * block]
+                turned = jnp.transpose(field.reshape(block, block), (1, 0))
                 o_nat[c, 0, x, :, hs] = turned
                 total = total + f_nat[c, 0, x, :, hs].astype(jnp.float32) * turned.astype(
                     jnp.float32
@@ -278,7 +270,6 @@
             return carry
 
         lax.fori_loop(0, rows, one_row, 0)
-        keep(h).start()
 
     def edges_out(g):
         rs = span(g)
@@ -290,7 +281,7 @@
         scale = gq[rs, :]
         for c in range(2):
             ls = slice(c * block, (c + 1) * block)
-            v = [vin[x, rs, ls].astype(jnp.float32) for x in range(rows)]
+            v = [vin[g, x, :, ls].astype(jnp.float32) for x in range(rows)]
             for x in range(rows):
                 total = beside(v[x])
                 if x > 0:
@@ -301,18 +292,18 @@
                 low = w.astype(jnp.bfloat16)
                 if x == 0:
                     part[0, rs, ls] = w
-                    hsend[0, 1, rs, ls] = low
-                    hsend[0, 0, rs, ls] = vin[0, rs, ls]
+                    hsend[g, 0, 1, :, ls] = low
+                    hsend[g, 0, 0, :, ls] = vin[g, 0, :, ls]
                 elif x == rows - 1:
                     part[1, rs, ls] = w
-                    hsend[1, 1, rs, ls] = low
-                    hsend[1, 0, rs, ls] = vin[rows - 1, rs, ls]
+                    hsend[g, 1, 1, :, ls] = low
+                    hsend[g, 1, 0, :, ls] = vin[g, rows - 1, :, ls]
                 else:
                     wext[2 + x, rs, ls] = low
                     if x == 1:
-                        hsend[0, 2, rs, ls] = low
+                        hsend[g, 0, 2, :, ls] = low
                     if x == rows - 2:
-                        hsend[1, 2, rs, ls] = low
+                        hsend[g, 1, 2, :, ls] = low
 
         @pl.when(send_left)
         def _():
@@ -349,20 +340,20 @@
             scale = gq[rs, :]
             for c in range(2):
                 ls = slice(c * block, (c + 1) * block)
-                near = hrecv[0, 0, rs, ls].astype(jnp.float32)
+                near = hrecv[g, 0, 0, :, ls].astype(jnp.float32)
                 wext[2, rs, ls] = (part[0, rs, ls] - scale * near).astype(jnp.bfloat16)
-                near = hrecv[1, 0, rs, ls].astype(jnp.float32)
+                near = hrecv[g, 1, 0, :, ls].astype(jnp.float32)
                 wext[rows + 1, rs, ls] = (part[1, rs, ls] - scale * near).astype(jnp.bfloat16)
-                mine = vin[0, rs, ls].astype(jnp.float32) * left_on
-                wext[1, rs, ls] = (hrecv[0, 1, rs, ls].astype(jnp.float32) - scale * mine).astype(
+                mine = vin[g, 0, :, ls].astype(jnp.float32) * left_on
+                wext[1, rs, ls] = (hrecv[g, 0, 1, :, ls].astype(jnp.float32) - scale * mine).astype(
                     jnp.bfloat16
                 )
-                mine = vin[rows - 1, rs, ls].astype(jnp.float32) * right_on
+                mine = vin[g, rows - 1, :, ls].astype(jnp.float32) * right_on
                 wext[rows + 2, rs, ls] = (
-                    hrecv[1, 1, rs, ls].astype(jnp.float32) - scale * mine
+                    hrecv[g, 1, 1, :, ls].astype(jnp.float32) - scale * mine
                 ).astype(jnp.bfloat16)
-                wext[0, rs, ls] = hrecv[0, 2, rs, ls]
-                wext[rows + 3, rs, ls] = hrecv[1, 2, rs, ls]
+                wext[0, rs, ls] = hrecv[g, 0, 2, :, ls]
+                wext[rows + 3, rs, ls] = hrecv[g, 1, 2, :, ls]
 
         def field_row(x):
             acc = None
@@ -374,7 +365,7 @@
                 )
                 acc = term if acc is None else acc + term
             row = acc.astype(jnp.bfloat16)
-            vout[x, rs, :] = row
+            vout[g, x, :, :] = row
             return row
 
         def near_only():
@@ -387,17 +378,17 @@
             v = [field_row(edge + i * inward) for i in range(3)]
             scale = gq_next[rs, :]
             first = 0 if inward > 0 else 1
-            fsend[0, rs, :] = v[0]
+            fsend[g, 0, :, :] = v[0]
             for c in range(2):
                 ls = slice(c * block, (c + 1) * block)
                 v0, v1, v2 = (row[:, ls].astype(jnp.float32) for row in v)
                 source = s_next[first, rs, ls].astype(jnp.float32)
-                fsend[1, rs, ls] = (source - scale * (v1 + beside(v0))).astype(jnp.bfloat16)
+                fsend[g, 1, :, ls] = (source - scale * (v1 + beside(v0))).astype(jnp.bfloat16)
                 source = s_next[1 - first, rs, ls].astype(jnp.float32)
-                fsend[2, rs, ls] = (source - scale * (v0 + v2 + beside(v1))).astype(jnp.bfloat16)
-            to_partner(g).start()
+                fsend[g, 2, :, ls] = (source - scale * (v0 + v2 + beside(v1))).astype(jnp.bfloat16)
             for i in range(3, rows):
                 field_row(edge + i * inward)
+            to_partner(g).start()
 
         @pl.when(far_left & has_below)
         def _():
@@ -419,7 +410,7 @@
         edges_out(g)
         return carry
 
-    depth = jnp.where(is_far & (t != tiles // 2) & (t != tiles // 2 - 1), 1, DEPTH)
+    depth = jnp.where(is_pair, 2, jnp.where(is_far, 0, 2))
     ahead = jnp.where(top, chunks, depth)
     lax.fori_loop(0, jnp.where(top, chunks, 0), first_edges, 0)
 
@@ -470,8 +461,6 @@
             finish(h)
 
     finish(halves - 1)
-    grad_copy = pltpu.make_async_copy(grad, grad_hbm, out_sem.at[halves])
-    grad_copy.start()
 
 
     @pl.when(is_far & has_above)
@@ -506,31 +495,21 @@
         return carry
 
     lax.fori_loop(0, chunks, drain, 0)
-    for h in range(halves):
-        keep(h).wait()
-    grad_copy.wait()
-
-
-def copy_kernel(adjoint_in, gradient_in, adjoint_out, gradient_out, held, held_gradient, sem):
+
+
+def copy_kernel(adjoint_in, gradient_in, adjoint_out, gradient_out, sem):
     rows = adjoint_in.shape[2]
-    pieces = [(gradient_in, held_gradient, gradient_out)]
+    copies = [pltpu.make_async_copy(gradient_in, gradient_out, sem.at[2 * rows])]
     for c in range(2):
         for x in range(rows):
-            pieces.append((adjoint_in.at[c, 0, x], held.at[c, x], adjoint_out.at[c, 0, x]))
-    fetched = [
-        pltpu.make_async_copy(source, here, sem.at[0, i])
-        for i, (source, here, _) in enumerate(pieces)
-    ]
-    stored = [
-        pltpu.make_async_copy(here, target, sem.at[1, i])
-        for i, (_, here, target) in enumerate(pieces)
-    ]
-    for copy in fetched:
+            copies.append(
+                pltpu.make_async_copy(
+                    adjoint_in.at[c, 0, x], adjoint_out.at[c, 0, x], sem.at[c * rows + x]
+                )
+            )
+    for copy in copies:
         copy.start()
-    for fetch, store in zip(fetched, stored):
-        fetch.wait()
-        store.start()
-    for copy in stored:
+    for copy in copies:
         copy.wait()
 
 
@@ -543,6 +522,7 @@
     bf16 = jnp.bfloat16
     f32 = jnp.float32
     hbm_spec = pl.BlockSpec(memory_space=pltpu.HBM)
+    vmem_spec = pl.BlockSpec(memory_space=pltpu.VMEM)
     index = jnp.transpose(factor_index, (2, 0, 1))
     thickness = pml_thickness[None]
     outs = (
@@ -553,27 +533,25 @@
         functools.partial(sweep_kernel, sweeps, tiles),
         out_shape=outs,
         in_specs=[hbm_spec] * 5,
-        out_specs=(hbm_spec, hbm_spec),
+        out_specs=(vmem_spec, vmem_spec),
         scratch_shapes=[
             pltpu.SMEM(index.shape, jnp.int32),
             pltpu.VMEM(thickness.shape, jnp.int32),
             pltpu.VMEM(adjoint_source.shape, bf16),
             pltpu.VMEM(forward_field.shape, bf16),
-            pltpu.VMEM(adjoint_source.shape, bf16),
-            pltpu.VMEM((1, rows, block), f32),
             pltpu.VMEM(factor_blocks.shape, bf16),
             pltpu.VMEM((rows, rhs, wide), bf16),
             pltpu.VMEM((2, rhs, wide), bf16),
             pltpu.VMEM((rhs, block), f32),
             pltpu.VMEM((rhs, block), f32),
             pltpu.VMEM((rows, nonzero, wide, wide), bf16),
-            pltpu.VMEM((rows, rhs, wide), bf16),
-            pltpu.VMEM((rows, rhs, wide), bf16),
+            pltpu.VMEM((chunks, rows, CHUNK, wide), bf16),
+            pltpu.VMEM((chunks, rows, CHUNK, wide), bf16),
             pltpu.VMEM((2, rhs, wide), f32),
             pltpu.VMEM((rows + 4, rhs, wide), bf16),
-            pltpu.VMEM((2, 3, rhs, wide), bf16),
-            pltpu.VMEM((3, rhs, wide), bf16),
-            pltpu.VMEM((2, 3, rhs, wide), bf16),
+            pltpu.VMEM((chunks, 2, 3, CHUNK, wide), bf16),
+            pltpu.VMEM((chunks, 3, CHUNK, wide), bf16),
+            pltpu.VMEM((chunks, 2, 3, CHUNK, wide), bf16),
             pltpu.SemaphoreType.DMA((5,)),
             pltpu.SemaphoreType.DMA((2,)),
             pltpu.SemaphoreType.DMA((chunks,)),
@@ -582,24 +560,23 @@
             pltpu.SemaphoreType.DMA((2, chunks)),
             pltpu.SemaphoreType.DMA((chunks,)),
             pltpu.SemaphoreType.DMA((chunks,)),
-            pltpu.SemaphoreType.DMA((rhs // block + 1,)),
-            pltpu.VMEM((2, rhs, wide), bf16),
+            pltpu.VMEM((chunks, 2, CHUNK, wide), bf16),
             pltpu.SemaphoreType.DMA((4, chunks)),
         ],
         compiler_params=pltpu.CompilerParams(
-            collective_id=0, has_side_effects=True, vmem_limit_bytes=63 * 1024 * 1024
+            collective_id=0, has_side_effects=True, vmem_limit_bytes=32 * 1024 * 1024
         ),
-    )(index, thickness, adjoint_source, factor_blocks, forward_field)
+    )(*(
+        pltpu.with_memory_space_constraint(operand, pltpu.HBM)
+        for operand in (index, thickness, adjoint_source, factor_blocks, forward_field)
+    ))
     return pl.pallas_call(
         copy_kernel,
         out_shape=outs,
-        in_specs=[hbm_spec] * 2,
+        in_specs=[vmem_spec] * 2,
         out_specs=(hbm_spec, hbm_spec),
-        scratch_shapes=[
-            pltpu.VMEM((2, rows, block, rhs), bf16),
-            pltpu.VMEM((1, rows, block), f32),
-            pltpu.SemaphoreType.DMA((2, 2 * rows + 1)),
-        ],
+        scratch_shapes=[pltpu.SemaphoreType.DMA((2 * rows + 1,))],
+        compiler_params=pltpu.CompilerParams(vmem_limit_bytes=4 * 1024 * 1024),
     )(*fields)
 
 

time: 96 us -> 94.1 us (0.980)
  Pallas kernels: 95.2 us -> 93.3 us
    pallas_call x1, Pallas kernels: 1.85 us -> 0.86 us  [on_device(): pl.pallas_call(copy_kernel, out_shape=outs, in_specs=[vmem_spec] * 2, out...]
where the time goes in v4:
time: 94.1 us; the launch traced here: 93.9 us
  Pallas kernels  93.3 us (99%)
    pallas_call x1, Pallas kernels, on_device(): pl.pallas_call(functools.partial(sweep_kernel, sweeps, tiles), out_shape=...  92.4 us

profile of v4, /device:TPU:31, one launch (start us, length us, event | category | flops | bytes accessed | tf_op | source)
XLA Modules:
  0.0 93.9 jit_solution(6257817427687234701)
XLA Ops:
  0.6 92.4 %shard_map.68 = (bf16[2,1,4,128,256]{4,3,2,1,0:T(8,128)(2,1)S(1)}, f32[1,4,128]{2,1,0:T(4,128)S(1)}) custom-call(s32[3,1,4]{2,1,0:T(1,128)} %bitcast.2, s32[1,256]{1,0:T(1,128)} %bitcast.3, bf16[2,1,4,128,256]{4,3,2,1,0:T(8,128)(2,1)} %src_hbm.1, bf16[1,4,3,2,128,128]{5,4,3,2,1,0:T(8,128)(2,1)} %fac_hbm.1, bf16[2,1,4,128,256]{4,3,2,1,0:T(8,128)(2,1)} %fwd_hbm.1), custom_call_target="tpu_custom_call" | custom-call | tf_op jit(solution)/shard_map/pallas_call | solution.py:532
  93.1 0.9 shard_map.69

commit v5 on v4

--- a/solution.py
+++ b/solution.py
@@ -191,12 +191,13 @@
     def span(g):
         return pl.ds(pl.multiple_of(g * CHUNK, CHUNK), CHUNK)
 
-    def hand_down(g):
+    def hand_down(g, half):
+        some = pl.ds(half * (rows // 2), rows // 2)
         return pltpu.make_async_remote_copy(
-            src_ref=vout.at[g],
-            dst_ref=vin.at[g],
-            send_sem=zsend_sem.at[g],
-            recv_sem=zrecv_sem.at[g],
+            src_ref=vout.at[g, some],
+            dst_ref=vin.at[g, some],
+            send_sem=zsend_sem.at[half, g],
+            recv_sem=zrecv_sem.at[half, g],
             device_id={"sweep": below},
         )
 
@@ -276,7 +277,8 @@
 
         @pl.when(has_above)
         def _():
-            hand_down(g).wait_recv()
+            hand_down(g, 0).wait_recv()
+            hand_down(g, 1).wait_recv()
 
         scale = gq[rs, :]
         for c in range(2):
@@ -370,7 +372,14 @@
 
         def near_only():
             settle()
-            for x in range(rows):
+            for x in range(rows // 2):
+                field_row(x)
+
+            @pl.when(has_below)
+            def _():
+                hand_down(g, 0).start()
+
+            for x in range(rows // 2, rows):
                 field_row(x)
 
         def with_far(edge, inward):
@@ -402,9 +411,13 @@
         def _():
             near_only()
 
+        @pl.when(is_far & has_below)
+        def _():
+            hand_down(g, 0).start()
+
         @pl.when(has_below)
         def _():
-            hand_down(g).start()
+            hand_down(g, 1).start()
 
     def first_edges(g, carry):
         edges_out(g)
@@ -470,7 +483,8 @@
     def drain(g, carry):
         @pl.when(has_below)
         def _():
-            hand_down(g).wait_send()
+            hand_down(g, 0).wait_send()
+            hand_down(g, 1).wait_send()
 
         @pl.when(is_far & has_below)
         def _():
@@ -554,8 +568,8 @@
             pltpu.VMEM((chunks, 2, 3, CHUNK, wide), bf16),
             pltpu.SemaphoreType.DMA((5,)),
             pltpu.SemaphoreType.DMA((2,)),
-            pltpu.SemaphoreType.DMA((chunks,)),
-            pltpu.SemaphoreType.DMA((chunks,)),
+            pltpu.SemaphoreType.DMA((2, chunks)),
+            pltpu.SemaphoreType.DMA((2, chunks)),
             pltpu.SemaphoreType.DMA((2, chunks)),
             pltpu.SemaphoreType.DMA((2, chunks)),
             pltpu.SemaphoreType.DMA((chunks,)),

time: 94.1 us -> 94.7 us (level)
  no operation moved by 1% of the time
where the time goes in v5:
time: 94.7 us; the launch traced here: 94.5 us
  Pallas kernels  93.9 us (99%)
    pallas_call x1, Pallas kernels, on_device(): pl.pallas_call(functools.partial(sweep_kernel, sweeps, tiles), out_shape=...  93 us

profile of v5, /device:TPU:31, one launch (start us, length us, event | category | flops | bytes accessed | tf_op | source)
XLA Modules:
  0.0 94.5 jit_solution(4512889572490966420)
XLA Ops:
  0.6 93.0 %shard_map.68 = (bf16[2,1,4,128,256]{4,3,2,1,0:T(8,128)(2,1)S(1)}, f32[1,4,128]{2,1,0:T(4,128)S(1)}) custom-call(s32[3,1,4]{2,1,0:T(1,128)} %bitcast.2, s32[1,256]{1,0:T(1,128)} %bitcast.3, bf16[2,1,4,128,256]{4,3,2,1,0:T(8,128)(2,1)} %src_hbm.1, bf16[1,4,3,2,128,128]{5,4,3,2,1,0:T(8,128)(2,1)} %fac_hbm.1, bf16[2,1,4,128,256]{4,3,2,1,0:T(8,128)(2,1)} %fwd_hbm.1), custom_call_target="tpu_custom_call" | custom-call | tf_op jit(solution)/shard_map/pallas_call | solution.py:546
  93.7 0.9 shard_map.69
